TPU v7x, 512 devices: a whole 4x8x8 slice. The times are simulated.
512 devices in a mesh: ctx: 64 (over z, x, core), head: 8 (over y).
Axes of the slice: x: 4, y: 8, z: 8, core: 2. Of those that a mesh axis runs over, the one named last changes fastest.
Arguments:
- query_raw: bfloat16 [8192, 2048], P('ctx', 'head'), may hold values from -6 to 6
- key_raw: bfloat16 [8192, 2048], P('ctx', 'head'), may hold values from -6 to 6
- value_raw: bfloat16 [8192, 4096], P('ctx', 'head'), may hold values from -6 to 6
- query_key_conv: bfloat16 [2, 4, 2048], P(None, None, 'head'), may hold values from -3 to 3
- value_conv: bfloat16 [4, 4096], P(None, 'head'), may hold values from -3 to 3
- output_gate: bfloat16 [8192, 4096], P('ctx', 'head'), may hold values from -6 to 6
- beta_logit: float32 [8192, 32], P('ctx', 'head')
- gate_logit: float32 [8192, 32], P('ctx', 'head')
- log_rate: float32 [32], P('head')
- norm_gain: float32 [128], replicated, may hold values from 0.5 to 2
- out_weight: bfloat16 [4096, 2048], P('head'), may hold values from -0.09375 to 0.09375
Outputs:
- mixed: bfloat16 [8192, 2048], P(('ctx', 'head'))
All inputs are finite; a program needn't handle non-finite values.
Results may differ from a plain program's by a relative error of at most 0.022.
Values may be sent and summed in bfloat16 or wider, within the bound.
No kernel may reach another device: no remote copies, remote signals or barrier semaphores. Data moves between devices by JAX's collectives and lax.ppermute only.
A program may use at most 128 MiB of HBM per device.

v0:
```python
import jax
import jax.numpy as jnp
from jax import lax
from jax.sharding import PartitionSpec as P

HDIM = 128
CONV = 4
SPAN = 128


def from_behind(value, axis, by):
    devices = lax.axis_size(axis)
    pairs = [(i, i + by) for i in range(devices) if 0 <= i + by < devices]
    return lax.ppermute(value, axis, pairs)


def prefix_2(value, axis, join, neutral):
    place = lax.axis_index(axis)
    gathered = jax.tree.map(
        lambda a, kind: lax.all_gather(a.astype(kind), axis), value, (jnp.bfloat16, jnp.bfloat16)
    )
    state = jax.tree.map(lambda a, e: jnp.zeros_like(a) + jnp.asarray(e, a.dtype), value, neutral)

    def one(lap, state):
        return join(
            state,
            jax.tree.map(
                lambda a, own: lax.dynamic_index_in_dim(a, lap, 0, False).astype(own.dtype),
                gathered,
                value,
            ),
        )

    return lax.fori_loop(0, place, one, state)


def conv_block(raw_rows, rim_rows, taps):
    length = raw_rows.shape[0]
    extended = jnp.concatenate([rim_rows, raw_rows], axis=0).astype(jnp.float32)
    total = jnp.zeros((length, raw_rows.shape[1]), jnp.float32)
    for offset in range(CONV):
        total = total + taps[offset].astype(jnp.float32) * extended[offset : offset + length]
    return jax.nn.silu(total)


def unit_rows(values):
    return values / jnp.sqrt(jnp.sum(values * values, axis=-1, keepdims=True) + 1e-06)


def local(
    query_raw,
    key_raw,
    value_raw,
    query_key_conv,
    value_conv,
    output_gate,
    beta_logit,
    gate_logit,
    log_rate,
    norm_gain,
    out_weight,
):
    highest_precision = lax.Precision.HIGHEST
    length = query_raw.shape[0]
    qk_width = query_raw.shape[1]
    v_width = value_raw.shape[1]
    key_heads = qk_width // HDIM
    value_heads = v_width // HDIM
    ratio = value_heads // key_heads
    blocks = length // SPAN
    keep = CONV - 1
    rim_rows = jnp.concatenate(
        [query_raw[length - keep :], key_raw[length - keep :], value_raw[length - keep :]], axis=1
    )
    earlier = from_behind(rim_rows, "ctx", 1)
    query = conv_block(query_raw, earlier[:, :qk_width], query_key_conv[0]).reshape(
        length, key_heads, HDIM
    )
    keyed = conv_block(key_raw, earlier[:, qk_width : 2 * qk_width], query_key_conv[1]).reshape(
        length, key_heads, HDIM
    )
    value = conv_block(value_raw, earlier[:, 2 * qk_width :], value_conv).reshape(
        length, value_heads, HDIM
    )
    query = jnp.repeat(unit_rows(query) * HDIM ** (-0.5), ratio, axis=1)
    keyed = jnp.repeat(unit_rows(keyed), ratio, axis=1)
    beta = jax.nn.sigmoid(beta_logit)
    decay = -jnp.exp(log_rate)[None, :] * jax.nn.softplus(gate_logit)

    def to_blocks(values):
        return values.reshape(blocks, SPAN, value_heads, HDIM).transpose(2, 0, 1, 3)

    query_blk = to_blocks(query)
    key_blk = to_blocks(keyed)
    value_blk = to_blocks(value)
    beta_blk = beta.reshape(blocks, SPAN, value_heads).transpose(2, 0, 1)
    gamma = jnp.cumsum(decay.reshape(blocks, SPAN, value_heads).transpose(2, 0, 1), axis=-1)
    relative = gamma[..., :, None] - gamma[..., None, :]
    position_list = jnp.arange(SPAN)
    below = position_list[:, None] > position_list[None, :]
    upto = position_list[:, None] >= position_list[None, :]
    strict_decay = jnp.where(below, jnp.exp(jnp.where(below, relative, 0.0)), 0.0)
    within_decay = jnp.where(upto, jnp.exp(jnp.where(upto, relative, 0.0)), 0.0)
    key_key = jnp.einsum("hncd,hnsd->hncs", key_blk, key_blk, precision=highest_precision)
    lower_part = strict_decay * key_key * beta_blk[..., None, :]
    system = jnp.eye(SPAN, dtype=jnp.float32) + lower_part
    growth = jnp.exp(gamma)[..., None]
    right_side = jnp.concatenate([value_blk, growth * key_blk], axis=-1)
    solved = lax.linalg.triangular_solve(
        system, right_side, left_side=True, lower=True, unit_diagonal=True
    )
    fresh = solved[..., :HDIM]
    wy_keys = solved[..., HDIM:]
    query_key = jnp.einsum("hncd,hnsd->hncs", query_blk, key_blk, precision=highest_precision)
    scores = within_decay * query_key * beta_blk[..., None, :]
    local_out = jnp.einsum("hncs,hnsv->hncv", scores, fresh, precision=highest_precision)
    lifted = growth * query_blk - jnp.einsum(
        "hncs,hnsk->hnck", scores, wy_keys, precision=highest_precision
    )
    tail_weight = (jnp.exp(gamma[..., -1:] - gamma) * beta_blk)[..., None] * key_blk
    identity_map = jnp.eye(HDIM, dtype=jnp.float32)
    transition = jnp.exp(gamma[..., -1])[..., None, None] * identity_map - jnp.einsum(
        "hnck,hncj->hnkj", tail_weight, wy_keys, precision=highest_precision
    )
    pushed = jnp.einsum("hnck,hncv->hnkv", tail_weight, fresh, precision=highest_precision)

    def matmul(left, right):
        return jnp.einsum("hij,hjk->hik", left, right, precision=highest_precision)

    def compose(carried, item):
        product, memory_state = carried
        step_map, step_push = item
        return (
            (matmul(step_map, product), matmul(step_map, memory_state) + step_push),
            (product, memory_state),
        )

    start_map = jnp.broadcast_to(identity_map, (value_heads, HDIM, HDIM))
    start_state = jnp.zeros((value_heads, HDIM, HDIM), jnp.float32)
    block_items = (transition.transpose(1, 0, 2, 3), pushed.transpose(1, 0, 2, 3))
    (shard_map_total, shard_state), (maps_before, states_before) = lax.scan(
        compose, (start_map, start_state), block_items
    )

    def combine(first, second):
        return (matmul(second[0], first[0]), matmul(second[0], first[1]) + second[1])

    prefix = prefix_2((shard_map_total, shard_state), "ctx", combine, (start_map, start_state))

    def sweep(memory_state, item):
        raised_block, block_local, step_map, step_push = item
        layer_output = block_local + jnp.einsum(
            "msq,mqz->msz", raised_block, memory_state, precision=highest_precision
        )
        return (matmul(step_map, memory_state) + step_push, layer_output)

    sweep_items = (
        lifted.transpose(1, 0, 2, 3),
        local_out.transpose(1, 0, 2, 3),
        block_items[0],
        block_items[1],
    )
    _, outputs = lax.scan(sweep, prefix[1], sweep_items)
    core = outputs.transpose(1, 0, 2, 3)
    core = core.transpose(1, 2, 0, 3).reshape(length, value_heads, HDIM)
    meansq = jnp.mean(core * core, axis=-1, keepdims=True)
    gate = jax.nn.silu(output_gate.reshape(length, value_heads, HDIM).astype(jnp.float32))
    normed = (
        (core / jnp.sqrt(meansq + 1e-06) * norm_gain * gate)
        .astype(jnp.bfloat16)
        .reshape(length, v_width)
    )
    return lax.psum_scatter(
        jnp.dot(normed, out_weight, preferred_element_type=jnp.float32).astype(jnp.bfloat16),
        "head",
        scatter_dimension=0,
        tiled=True,
    )


def solution(mesh):
    in_specs = (
        P("ctx", "head"),
        P("ctx", "head"),
        P("ctx", "head"),
        P(None, None, "head"),
        P(None, "head"),
        P("ctx", "head"),
        P("ctx", "head"),
        P("ctx", "head"),
        P("head"),
        P(),
        P("head", None),
    )
    out_specs = P(("ctx", "head"), None)
    return jax.shard_map(local, mesh=mesh, in_specs=in_specs, out_specs=out_specs, check_vma=False)
```

profile of v0, /device:TPU:6, one launch (start us, length us, event | category | flops | bytes accessed | tf_op | source)
XLA Modules:
  0.0 379.8 jit_solution(533023530290723329)
XLA Ops:
  6.5 0.9 slice.125
  7.4 0.7 slice.124
  8.1 0.7 slice.123
  8.8 0.2 copy.38
  9.0 1.9 collective-permute-start
  10.9 0.7 fusion.60
  11.6 0.7 add_divide_fusion
  12.3 0.9 slice_convert_fusion.7
  13.2 0.7 exponential_negate_fusion
  13.9 0.7 fusion.43
  14.6 1.2 reduce_window_sum.11
  15.8 0.2 slice_reduce_fusion
  16.0 0.9 slice_convert_fusion.3
  16.9 0.1 iota_compare_fusion.1
  17.0 0.1 exponential_multiply_fusion
  17.1 0.0 copy-start.1
  17.1 1.0 copy.43
  18.1 0.6 exp.72
  18.7 0.1 copy.39
  18.8 0.9 maximum_convert_fusion.1
  19.7 0.1 divide_multiply_fusion.3
  19.8 0.1 reshape.271
  19.9 0.2 multiply_reduce_fusion.1
  20.1 0.2 divide_multiply_fusion.2
  20.4 0.1 copy.41
  20.5 0.9 maximum_convert_fusion.2
  21.3 0.1 divide_multiply_fusion.1
  21.4 0.1 reshape.273
  21.5 0.2 multiply_reduce_fusion
  21.8 0.2 broadcast_divide_fusion
  22.0 0.1 maximum_convert_fusion
  22.2 0.6 divide_multiply_fusion
  22.7 0.1 copy.44
  22.9 0.7 fusion.8
  23.6 39.9 %custom-call.3 = f32[4,1,1,128,128]{3,4,2,1,0:T(8,128)} custom-call(f32[4,1,1,128,128]{4,3,2,1,0:T(8,128)S(1)} %fusion.8), custom_call_target="InvertDiagBlocksLowerTriangular" | custom-call | tf_op jit(solution)/shard_map/triangular_solve | solution.py:109
  63.5 0.9 bitcast_multiply_fusion.1
  64.4 1.6 convolution_bitcast_fusion
  66.0 1.4 convolution_subtract_fusion
  67.4 1.9 convolution_convert_fusion.1
  69.3 0.0 all-gather.5.cloned.1.call-update
  69.3 0.0 all-gather.7.cloned.1.call-start
  69.4 0.3 fusion.39
  69.7 1.3 fusion.11
  71.0 0.0 all-gather.7.cloned.1.call-update
  71.0 0.0 reduce-scatter.2.cloned.1.call-start
  71.1 1.0 copy.50
  72.1 0.7 broadcast_bitcast_fusion
  72.8 0.7 fusion.4
  73.5 1.3 fusion.10
  74.8 0.6 fusion.31
  75.4 87.5 %all-gather.5.cloned.1.call-done = bf16[256,128,128]{2,1,0:T(8,128)(2,1)} async-done(((bf16[4,128,128]{2,1,0:T(8,128)(2,1)}), bf16[256,128,128]{2,1,0:T(8,128)(2,1)}) %all-gather.5.cloned.1.call-update) | async-done | bytes 8388624 | tf_op jit(solution)/shard_map/all_gather | solution.py:20
  162.9 89.3 %all-gather.7.cloned.1.call-done = bf16[256,128,128]{2,1,0:T(8,128)(2,1)} async-done(((bf16[4,128,128]{2,1,0:T(8,128)(2,1)}), bf16[256,128,128]{2,1,0:T(8,128)(2,1)}) %all-gather.7.cloned.1.call-update) | async-done | bytes 8388624 | tf_op jit(solution)/shard_map/all_gather | solution.py:20
  252.3 7.9 %while.3 = (s32[]{:T(128)}, f32[4,128,128]{2,1,0:T(8,128)S(1)}, s32[]{:T(128)}, bf16[64,4,128,128]{3,2,1,0:T(8,128)(2,1)}, bf16[64,4,128,128]{3,2,1,0:T(8,128)(2,1)}, /*index=5*/s32[]{:T(128)}, s32[]{:T(128)}, s32[]{:T(128)}) while((s32[]{:T(128)}, f32[4,128,128]{2,1,0:T(8,128)S(1)}, s32[]{:T(128)}, bf16[64,4,128,128]{3,2,1,0:T(8,128)(2,1)}, ...), condition=%wide.region_4.5_spmd, body=%wide.region_3.4_spmd.sunk | while | flops 100794368 | bytes 1311871 | solution.py:34
  252.4 1.3 convolution_add_fusion.4
  253.7 1.3 convolution_add_fusion.4
  255.0 1.3 convolution_add_fusion.4
  256.3 1.3 convolution_add_fusion.4
  257.6 1.3 convolution_add_fusion.4
  258.9 1.3 convolution_add_fusion.4
  260.2 0.6 fusion.26
  260.8 0.1 fusion.30
  261.0 1.3 convolution_convert_fusion
  262.2 0.0 reduce-scatter.2.cloned.1.call-update
  262.3 111.1 %reduce-scatter.2.cloned.1.call-done = bf16[16,2048]{1,0:T(8,128)(2,1)} async-done(((bf16[128,2048]{1,0:T(8,128)(2,1)}), bf16[16,2048]{1,0:T(8,128)(2,1)}) %reduce-scatter.2.cloned.1.call-update) | async-done | bytes 65552 | tf_op jit(solution)/shard_map/reduce_scatter | solution.py:173
  (26 shorter events, 0.3 us)
Async XLA Ops:
  6.5 254.4 %copy-start = (bf16[512,2048]{1,0:T(8,128)(2,1)S(1)}, bf16[512,2048]{1,0:T(8,128)(2,1)}, u32[]{:S(2)}) copy-start(bf16[512,2048]{1,0:T(8,128)(2,1)} %param.23) | copy-start | bytes 6291460
  6.5 156.4 %all-gather.5.cloned.1.call-start = ((), (), s32[]{:S(2)}) async-start(), calls=%async_computation.2 | async-start | bytes 8519680 | tf_op jit(solution)/shard_map/all_gather | solution.py:20
  9.0 9.7 %collective-permute-start = (bf16[3,1024]{0,1:T(8,128)(2,1)S(1)}, bf16[3,1024]{0,1:T(8,128)(2,1)S(1)}, u32[]{:S(2)}, u32[]{:S(2)}) collective-permute-start(bf16[3,1024]{0,1:T(8,128)(2,1)S(1)} %copy.38), channel_id=1, source_target_pairs={{0,8},{8,16},{16,24},{24,32},{32,40},{40,48},{48,56},{56,64},{64,7... | collective-permute-start | bytes 18440 | tf_op jit(solution)/shard_map/ppermute | solution.py:14
  17.1 47.4 %copy-start.1 = (f32[128,128]{1,0:T(8,128)}, f32[128,128]{1,0:T(8,128)S(1)}, u32[]{:S(2)}) copy-start(f32[128,128]{1,0:T(8,128)S(1)} %get-tuple-element.117) | copy-start | bytes 196612
  69.3 182.9 %all-gather.7.cloned.1.call-start = ((), (), s32[]{:S(2)}) async-start(), calls=%async_computation.3 | async-start | bytes 8519680 | tf_op jit(solution)/shard_map/all_gather | solution.py:20
  71.0 302.3 %reduce-scatter.2.cloned.1.call-start = ((), (), s32[]{:S(2)}) async-start(), calls=%async_computation.1 | async-start | bytes 589824 | tf_op jit(solution)/shard_map/reduce_scatter | solution.py:173
Sparse Core Ops, SparseCore 0:
  69.5 93.4 all-gather.4
  166.3 85.9 all-gather.6
  262.4 110.8 reduce-scatter.1
where the time goes:
time: 382 us; the launch traced here: 380 us
  waiting for transfers between devices  288 us (75%)
  other arithmetic  50.4 us (13%)
  matrix products  19.2 us (5%)
  between operations  13.4 us (4%)
  local copies, waits for them, and re-layouts  6.61 us (2%)
    all_gather x2, waiting for transfers between devices, prefix_2(): lax.all_gather(a.astype(kind), axis)  177 us
    reduce_scatter x1, waiting for transfers between devices, local(): lax.psum_scatter(jnp.dot(normed, out_weight, preferred_element_type=jnp.f...  111 us
    another operation x2, other arithmetic, local(): lax.linalg.triangular_solve(system, right_side, left_side=True, lower=Tru...  39.9 us
    dot_general x8, matrix products, matmul(): return jnp.einsum('hij,hjk->hik', left, right, precision=highest_precision)  9.75 us
  transfers between devices with their start and end apart: 4, of which 3 were waited for; matrix products, arithmetic and copies ran while one was open for 4% of the time, Pallas kernels for 0%

commit v1 on v0

v1 whole, which is shorter than its diff:
```python
import jax
import jax.numpy as jnp
from jax import lax
from jax.experimental import pallas as pl
from jax.experimental.pallas import tpu as pltpu
from jax.sharding import PartitionSpec as P

HDIM = 128
CONV = 4
SPAN = 128
GROUP = 4
ROW = 4
SLAB = 4
EXTRA = 16
INTERPRET = False
F32 = jnp.float32
BF16 = jnp.bfloat16
NN = (((1,), (0,)), ((), ()))
NT = (((1,), (1,)), ((), ()))
TN = (((0,), (0,)), ((), ()))


def split2(a):
    high = a.astype(BF16)
    return high, (a - high.astype(F32)).astype(BF16)


def split3(a):
    high = a.astype(BF16)
    rest = a - high.astype(F32)
    mid = rest.astype(BF16)
    return high, mid, (rest - mid.astype(F32)).astype(BF16)


def dot1(a, b, dims=NN):
    return lax.dot_general(a.astype(BF16), b.astype(BF16), dims, preferred_element_type=F32)


def dot3(a, b, dims=NN):
    a_high, a_low = split2(a)
    b_high, b_low = split2(b)
    return dot1(a_high, b_high, dims) + (dot1(a_high, b_low, dims) + dot1(a_low, b_high, dims))


def dot_mixed(a, b, dims=NN):
    b_high, b_low = split2(b)
    return dot1(a, b_high, dims) + dot1(a, b_low, dims)


def softplus(x):
    y = jnp.exp(-jnp.abs(x))
    u = 1.0 + y
    log1p = jnp.where(u == 1.0, y, jnp.log(u) * (y / jnp.where(u == 1.0, 1.0, u - 1.0)))
    return jnp.maximum(x, 0.0) + log1p


def silu(v):
    return v / (1.0 + jnp.exp(-v))


def pack_kernel(q_ref, k_ref, v_ref, beta_ref, gate_ref, rate_ref, msg_ref, *rim_refs):
    length = q_ref.shape[0]
    ratio = (v_ref.shape[1] // HDIM) // (q_ref.shape[1] // HDIM)
    beta = jax.nn.sigmoid(beta_ref[...])
    decay = -jnp.exp(rate_ref[...]) * softplus(gate_ref[...])
    lane = lax.broadcasted_iota(jnp.int32, (length, HDIM), 1)
    table = jnp.zeros((length, HDIM), F32)
    for at, values in ((0, beta), (3, decay)):
        for p, part in enumerate(split3(values)):
            part = part.astype(F32)
            for h in range(GROUP):
                table = jnp.where(lane == EXTRA * h + at + p, part[:, h : h + 1], table)
    table = table.T
    for h in range(GROUP):
        kh = h // ratio
        query = q_ref[:, kh * HDIM : (kh + 1) * HDIM]
        keyed = k_ref[:, kh * HDIM : (kh + 1) * HDIM]
        value = v_ref[:, h * HDIM : (h + 1) * HDIM]
        msg_ref[h, 0:length] = query
        msg_ref[h, length : 2 * length] = keyed
        msg_ref[h, 2 * length : 3 * length] = value
        msg_ref[h, 3 * length : 3 * length + EXTRA] = table[EXTRA * h : EXTRA * (h + 1)].astype(BF16)
        rim_refs[h][:, 0:HDIM] = query[length - 16 :]
        rim_refs[h][:, HDIM : 2 * HDIM] = keyed[length - 16 :]
        rim_refs[h][:, 2 * HDIM : 3 * HDIM] = value[length - 16 :]


def chunk_kernel(msg_ref, rim0, rim1, rim2, rim3, qk_taps_ref, v_taps_ref, map_ref, out_ref, lift_ref):
    length = SPAN
    total = GROUP * length
    place = lax.axis_index("ctx") % GROUP
    rims = [r[8:16, :].astype(F32) for r in (rim0, rim1, rim2, rim3)]
    rim = (rims[0] + rims[1]) + (rims[2] + rims[3])

    def pick(parts):
        got = parts[0]
        for i in range(1, len(parts)):
            got = jnp.where(place == i, parts[i], got)
        return got

    ratio = v_taps_ref.shape[1] // qk_taps_ref.shape[2]

    def taps_of(ref_part, repeat):
        heads = [ref_part[:, (h // repeat) * HDIM : (h // repeat + 1) * HDIM] for h in range(GROUP)]
        return pick([a.astype(F32) for a in heads])

    taps = (
        taps_of(qk_taps_ref[0], ratio),
        taps_of(qk_taps_ref[1], ratio),
        taps_of(v_taps_ref[...], 1),
    )

    def convolved(which):
        rows = [msg_ref[s, which * length : (which + 1) * length, :].astype(F32) for s in range(GROUP)]
        extended = jnp.concatenate([rim[:, which * HDIM : (which + 1) * HDIM]] + rows, axis=0)
        tap = taps[which]
        acc = tap[CONV - 1 : CONV] * extended
        for by in range(1, CONV):
            acc = acc + tap[CONV - 1 - by : CONV - by] * pltpu.roll(extended, by, 0)
        return silu(acc[8 : 8 + total])

    query = convolved(0)
    query = query * (lax.rsqrt(jnp.sum(query * query, axis=-1, keepdims=True) + 1e-06) * HDIM ** (-0.5))
    keyed = convolved(1)
    keyed = keyed * lax.rsqrt(jnp.sum(keyed * keyed, axis=-1, keepdims=True) + 1e-06)
    value = convolved(2)

    row = lax.broadcasted_iota(jnp.int32, (length, length), 0)
    col = lax.broadcasted_iota(jnp.int32, (length, length), 1)
    eye = jnp.where(row == col, 1.0, 0.0)
    lower = jnp.where(row >= col, 1.0, 0.0).astype(BF16)
    eye_b = eye.astype(BF16)
    chunks = range(GROUP)
    at = lambda a, c: a[c * length : (c + 1) * length]
    extra = [msg_ref[s, 3 * length : 3 * length + EXTRA, :] for s in chunks]
    extra_f = [e.astype(F32) for e in extra]
    beta_row = [e[0:1] + e[1:2] + e[2:3] for e in extra_f]
    extra_col = [dot1(eye_b, e, NT) for e in extra]
    beta_col = [e[:, 0:1] + e[:, 1:2] + e[:, 2:3] for e in extra_col]
    run_row = [dot1(e, lower, NT) for e in extra]
    run_col = [dot1(lower, e, NT) for e in extra]
    gamma_row = [e[3:4] + e[4:5] + e[5:6] for e in run_row]
    gamma_col = [e[:, 3:4] + e[:, 4:5] + e[:, 5:6] for e in run_col]
    gamma_end = [g[length - 1 :] for g in gamma_col]
    within = [
        jnp.where(row >= col, jnp.exp(jnp.where(row >= col, gamma_col[c] - gamma_row[c], 0.0)), 0.0)
        * beta_row[c]
        for c in chunks
    ]
    grow = [jnp.exp(g) for g in gamma_col]
    keys = [at(keyed, c) for c in chunks]
    queries = [at(query, c) for c in chunks]
    low = [jnp.where(row > col, within[c] * dot3(keys[c], keys[c], NT), 0.0) for c in chunks]
    inverse = [eye - jnp.where((row // 2) == (col // 2), low[c], 0.0) for c in chunks]
    size = 2
    while size < length:
        join = ((row // (2 * size)) == (col // (2 * size))) & ((row // size) > (col // size))
        step = [dot3(jnp.where(join, low[c], 0.0), inverse[c]) for c in chunks]
        inverse = [inverse[c] - dot3(inverse[c], step[c]) for c in chunks]
        size *= 2
    right = [jnp.concatenate([grow[c] * keys[c], at(value, c)], axis=1) for c in chunks]
    solved = [dot3(inverse[c], right[c]) for c in chunks]
    tail = [(jnp.exp(gamma_end[c] - gamma_col[c]) * beta_col[c]) * keys[c] for c in chunks]
    pushed = [dot3(tail[c], solved[c], TN) for c in chunks]
    steps = [jnp.exp(gamma_end[c]) * eye - pushed[c][:, :HDIM] for c in chunks]
    adds = [pushed[c][:, HDIM:] for c in chunks]
    before = [None]
    state = jnp.concatenate([steps[0], adds[0]], axis=1)
    for c in range(1, GROUP):
        before.append(state)
        moved = dot3(steps[c], state)
        state = jnp.concatenate([moved[:, :HDIM], moved[:, HDIM:] + adds[c]], axis=1)
    for s in range(map_ref.shape[0]):
        map_ref[s, 0:HDIM, :] = state[:, :HDIM].astype(BF16)
        map_ref[s, HDIM : 2 * HDIM, :] = state[:, HDIM:].astype(BF16)
    scores = [within[c] * dot3(queries[c], keys[c], NT) for c in chunks]
    local = [dot3(scores[c], solved[c]) for c in chunks]
    for c in chunks:
        lifted = grow[c] * queries[c] - local[c][:, :HDIM]
        own = local[c][:, HDIM:]
        if c:
            both = dot3(lifted, before[c])
            lifted = both[:, :HDIM]
            own = own + both[:, HDIM:]
        out_ref[c * length : (c + 1) * length, :] = own
        lift_ref[c * length : (c + 1) * length, :] = lifted.astype(BF16)


def chain_kernel(maps_ref, total_ref, mine_ref):
    place = (lax.axis_index("ctx") // GROUP) % ROW
    row = lax.broadcasted_iota(jnp.int32, (HDIM, 2 * HDIM), 0)
    col = lax.broadcasted_iota(jnp.int32, (HDIM, 2 * HDIM), 1)
    mine = jnp.where(row == col, 1.0, 0.0)
    state = jnp.concatenate([maps_ref[0, :HDIM, :], maps_ref[0, HDIM:, :]], axis=1).astype(F32)
    for i in range(1, ROW):
        mine = jnp.where(place == i, state, mine)
        moved = dot_mixed(maps_ref[i, :HDIM, :], state)
        state = jnp.concatenate(
            [moved[:, :HDIM], moved[:, HDIM:] + maps_ref[i, HDIM:, :].astype(F32)], axis=1
        )
    for s in range(SLAB):
        total_ref[s, :HDIM, :] = state[:, :HDIM].astype(BF16)
        total_ref[s, HDIM:, :] = state[:, HDIM:].astype(BF16)
    mine_ref[...] = mine


def finish_kernel(totals_ref, mine_ref, own_ref, lift_ref, gain_ref, normed_ref):
    place = lax.axis_index("ctx") // (GROUP * ROW)
    state = jnp.zeros((HDIM, HDIM), F32)
    got = state
    for i in range(1, SLAB):
        push = totals_ref[i - 1, HDIM:, :].astype(F32)
        state = push if i == 1 else dot_mixed(totals_ref[i - 1, :HDIM, :], state) + push
        got = jnp.where(place == i, state, got)
    start = dot3(mine_ref[:, :HDIM], got) + mine_ref[:, HDIM:]
    core = own_ref[...] + dot_mixed(lift_ref[...], start)
    mean = jnp.mean(core * core, axis=-1, keepdims=True)
    normed = (core * lax.rsqrt(mean + 1e-06) * gain_ref[...]).astype(BF16)
    for s in range(GROUP):
        normed_ref[s] = normed[s * SPAN : (s + 1) * SPAN]


def project_kernel(normed_ref, gate_ref, weight_ref, partial_ref):
    parts = []
    for h in range(GROUP):
        gate = silu(gate_ref[:, h * HDIM : (h + 1) * HDIM].astype(F32))
        parts.append((normed_ref[h].astype(F32) * gate).astype(BF16))
    left = jnp.concatenate(parts, axis=1)
    partial_ref[...] = lax.dot_general(
        left, weight_ref[...], NN, preferred_element_type=F32
    ).astype(BF16)


def call(body, outs, *args):
    return pl.pallas_call(
        body,
        out_shape=outs,
        compiler_params=pltpu.CompilerParams(vmem_limit_bytes=48 * 1024 * 1024),
        interpret=INTERPRET,
    )(*args)


def local(
    query_raw,
    key_raw,
    value_raw,
    query_key_conv,
    value_conv,
    output_gate,
    beta_logit,
    gate_logit,
    log_rate,
    norm_gain,
    out_weight,
):
    shape = jax.ShapeDtypeStruct
    devices = lax.axis_size("ctx")
    heads = lax.axis_size("head")
    length = query_raw.shape[0]
    width = out_weight.shape[1]
    near = [[GROUP * g + i for i in range(GROUP)] for g in range(devices // GROUP)]
    reach = GROUP * ROW
    rows = [
        [z * reach + GROUP * r + i for r in range(ROW)]
        for z in range(devices // reach)
        for i in range(GROUP)
    ]
    slabs = [[z * reach + i for z in range(SLAB)] for i in range(reach)]

    def trade(a, groups):
        return lax.all_to_all(a, "ctx", 0, 0, axis_index_groups=groups)

    message, *rims = call(
        pack_kernel,
        [shape((GROUP, 3 * length + EXTRA, HDIM), BF16)] + [shape((16, 3 * HDIM), BF16)] * GROUP,
        query_raw,
        key_raw,
        value_raw,
        beta_logit,
        gate_logit,
        log_rate.reshape(1, -1),
    )
    rims = [
        lax.ppermute(rim, "ctx", [(i, i + 1 + h) for i in range(GROUP - 1, devices - 1, GROUP)])
        for h, rim in enumerate(rims)
    ]
    message = trade(message, near)
    maps, own, lifted = call(
        chunk_kernel,
        [
            shape((ROW, 2 * HDIM, HDIM), BF16),
            shape((GROUP * SPAN, HDIM), F32),
            shape((GROUP * SPAN, HDIM), BF16),
        ],
        message,
        *rims,
        query_key_conv,
        value_conv,
    )
    maps = trade(maps, rows)
    totals, mine = call(
        chain_kernel,
        [shape((SLAB, 2 * HDIM, HDIM), BF16), shape((HDIM, 2 * HDIM), F32)],
        maps,
    )
    totals = trade(totals, slabs)
    normed = call(
        finish_kernel,
        shape((GROUP, SPAN, HDIM), BF16),
        totals,
        mine,
        own,
        lifted,
        norm_gain.reshape(1, -1),
    )
    normed = trade(normed, near)
    partial = call(project_kernel, shape((length, width), BF16), normed, output_gate, out_weight)
    partial = lax.all_to_all(partial.reshape(heads, length // heads, width), "head", 0, 0)
    return jnp.sum(partial.astype(F32), axis=0).astype(BF16)


def solution(mesh):
    in_specs = (
        P("ctx", "head"),
        P("ctx", "head"),
        P("ctx", "head"),
        P(None, None, "head"),
        P(None, "head"),
        P("ctx", "head"),
        P("ctx", "head"),
        P("ctx", "head"),
        P("head"),
        P(),
        P("head", None),
    )
    out_specs = P(("ctx", "head"), None)
    return jax.shard_map(local, mesh=mesh, in_specs=in_specs, out_specs=out_specs, check_vma=False)
```

time: 382 us -> 91.7 us (0.24)
  the two profiles are of different devices: /device:TPU:6 before, /device:TPU:2 now
where the time goes in v1:
time: 91.7 us; the launch traced here: 91.2 us
  blocking collectives  61.1 us (67%)
  starting transfers between devices  12 us (13%)
  Pallas kernels  7.66 us (8%)
  local copies, waits for them, and re-layouts  6.36 us (7%)
  waiting for transfers between devices  3.25 us (4%)
    all_to_all x3, blocking collectives, trade(): return lax.all_to_all(a, 'ctx', 0, 0, axis_index_groups=groups)  36.6 us
    all_to_all x1, blocking collectives, local(): lax.all_to_all(partial.reshape(heads, length // heads, width), 'head', 0, 0)  24.5 us
    all_to_all x1, starting transfers between devices, trade(): return lax.all_to_all(a, 'ctx', 0, 0, axis_index_groups=groups)  9.34 us
    pallas_call x5, Pallas kernels, call(): pl.pallas_call(body, out_shape=outs, compiler_params=pltpu.CompilerParams...  7.66 us
    unnamed x20, local copies, waits for them, and re-layouts  6.36 us
    all_to_all x1, waiting for transfers between devices, trade(): return lax.all_to_all(a, 'ctx', 0, 0, axis_index_groups=groups)  3.24 us
    ppermute x4, starting transfers between devices, local(): lax.ppermute(rim, 'ctx', [(i, i + 1 + h) for i in range(GROUP - 1, device...  2.64 us
  transfers between devices with their start and end apart: 5, of which 1 were waited for; matrix products, arithmetic and copies ran while one was open for 0% of the time, Pallas kernels for 0%

profile of v1, /device:TPU:2, one launch (start us, length us, event | category | flops | bytes accessed | tf_op | source)
XLA Modules:
  0.0 91.2 jit_solution(8068324278030386223)
XLA Ops:
  0.0 0.0 copy-start.8
  0.0 0.8 copy.12.beta_ref
  0.8 0.8 copy.13.gate_ref
  1.6 0.0 copy-start
  1.6 0.0 copy-start.1
  1.6 0.0 copy-start.2
  1.6 1.0 %copy-done.2 = bf16[128,512]{1,0:T(8,128)(2,1)S(1)} copy-done((bf16[128,512]{1,0:T(8,128)(2,1)S(1)}, bf16[128,512]{1,0:T(8,128)(2,1)}, u32[]{:S(2)}) %copy-start.2) | copy-done | bytes 131096
  2.7 0.0 copy-start.3
  2.7 0.8 copy-done.3
  3.5 0.0 copy-start.4
  3.5 0.8 copy-done.4
  4.3 0.0 copy-start.7
  4.3 0.7 copy-done.7
  5.0 1.2 %shard_map.109 = (bf16[4,400,128]{2,1,0:T(8,128)(2,1)}, bf16[16,384]{1,0:T(8,128)(2,1)S(1)}, bf16[16,384]{1,0:T(8,128)(2,1)S(1)}, bf16[16,384]{1,0:T(8,128)(2,1)S(1)}, bf16[16,384]{1,0:T(8,128)(2,1)S(1)}) custom-call(bf16[128,256]{1,0:T(8,128)(2,1)S(1)} %copy-done.3, bf16[128,256]{1,0:T(8,128)(2,1)S(1)} %copy-done.4, bf16[128,512]{1,0:T(8,128)(2,1)S(1)} %copy-done.2, ...), custom_call_target="tpu_custom_call" | custom-call | tf_op jit(solution)/shard_map/pallas_call | solution.py:235
  6.2 9.3 %all-to-all-start = ((bf16[4,400,128]{2,1,0:T(8,128)(2,1)}), bf16[4,400,128]{2,1,0:T(8,128)(2,1)S(1)}, u32[]{:S(2)}, u32[]{:S(2)}) async-start(bf16[4,400,128]{2,1,0:T(8,128)(2,1)} %get-tuple-element.15), calls=%async_computation | async-start | bytes 819200 | tf_op jit(solution)/shard_map/all_to_all | solution.py:271
  15.5 0.7 collective-permute-start
  16.2 0.7 collective-permute-start.1
  16.8 0.7 collective-permute-start.2
  17.5 0.7 collective-permute-start.3
  18.2 0.0 collective-permute-done.rim0
  18.2 0.0 collective-permute-done.1.rim1
  18.2 0.0 collective-permute-done.2.rim2
  18.2 0.0 collective-permute-done.3.rim3
  18.2 3.2 %all-to-all-done.msg_ref = bf16[4,400,128]{2,1,0:T(8,128)(2,1)S(1)} async-done(((bf16[4,400,128]{2,1,0:T(8,128)(2,1)}), bf16[4,400,128]{2,1,0:T(8,128)(2,1)S(1)}, u32[]{:S(2)}, u32[]{:S(2)}) %all-to-all-start) | async-done | bytes 409632 | tf_op jit(solution)/shard_map/all_to_all | solution.py:271
  21.4 0.0 copy-start.5
  21.5 0.7 copy-done.5
  22.1 0.0 copy-start.6
  22.1 0.7 copy-done.6
  22.8 4.6 %shard_map.110 = (bf16[4,256,128]{2,1,0:T(8,128)(2,1)S(1)}, f32[512,128]{1,0:T(8,128)S(1)}, bf16[512,128]{1,0:T(8,128)(2,1)S(1)}) custom-call(bf16[4,400,128]{2,1,0:T(8,128)(2,1)S(1)} %all-to-all-done.msg_ref, bf16[16,384]{1,0:T(8,128)(2,1)S(1)} %collective-permute-done.rim0, bf16[16,384]{1,0:T(8,128)(2,1)S(1)} %collective-permute-done.1.rim1, ...), custom_call_target="tpu_custom_call" | custom-call | tf_op jit(solution)/shard_map/pallas_call | solution.py:235
  27.5 11.4 %all_to_all.25.maps_ref = bf16[4,256,128]{2,1,0:T(8,128)(2,1)S(1)} all-to-all(bf16[4,256,128]{2,1,0:T(8,128)(2,1)S(1)} %get-tuple-element.20), channel_id=1, replica_groups={{0,32,64,96},{8,40,72,104},{16,48,80,112},{24,56,88,120},{128,160,192,2..., dimensions={0} | all-to-all | bytes 524288 | tf_op jit(solution)/shard_map/all_to_all | solution.py:271
  38.9 0.6 shard_map.111
  39.5 16.8 %all_to_all.26.totals_ref = bf16[4,256,128]{2,1,0:T(8,128)(2,1)S(1)} all-to-all(bf16[4,256,128]{2,1,0:T(8,128)(2,1)S(1)} %get-tuple-element.21), channel_id=1, replica_groups={{0,128,256,384},{8,136,264,392},{16,144,272,400},{24,152,280,408},{32,1..., dimensions={0} | all-to-all | bytes 524288 | tf_op jit(solution)/shard_map/all_to_all | solution.py:271
  56.3 0.0 copy-done.8
  56.3 0.8 shard_map.112
  57.1 8.4 %all_to_all.27.normed_ref = bf16[4,128,128]{2,1,0:T(8,128)(2,1)S(1)} all-to-all(bf16[4,128,128]{2,1,0:T(8,128)(2,1)S(1)} %shard_map.112), channel_id=1, replica_groups={{0,8,16,24},{32,40,48,56},{64,72,80,88},{96,104,112,120},{128,136,144,1..., dimensions={0} | all-to-all | bytes 262144 | tf_op jit(solution)/shard_map/all_to_all | solution.py:271
  65.5 0.0 copy-done
  65.5 0.0 copy-done.1
  65.5 0.5 shard_map.113
  66.0 24.5 %all_to_all.28 = bf16[8,16,2048]{2,1,0:T(8,128)(2,1)S(1)} all-to-all(bf16[8,16,2048]{2,1,0:T(8,128)(2,1)S(1)} %bitcast.3), channel_id=1, replica_groups=mesh['ctx'=64,'head'=8] {'head'}, dimensions={0} | all-to-all | bytes 1048576 | tf_op jit(solution)/shard_map/all_to_all | solution.py:318
  90.5 0.7 reduce_sum.12
Async XLA Ops:
  0.0 56.3 %copy-start.8 = (f32[128]{0:T(128)S(1)}, f32[128]{0:T(128)}, u32[]{:S(2)}) copy-start(f32[128]{0:T(128)} %param.20) | copy-start | bytes 1540
  1.6 63.9 %copy-start = (bf16[512,2048]{1,0:T(8,128)(2,1)S(1)}, bf16[512,2048]{1,0:T(8,128)(2,1)}, u32[]{:S(2)}) copy-start(bf16[512,2048]{1,0:T(8,128)(2,1)} %weight_ref.1) | copy-start | bytes 6291460
  1.6 63.9 %copy-start.1 = (bf16[128,512]{1,0:T(8,128)(2,1)S(1)}, bf16[128,512]{1,0:T(8,128)(2,1)}, u32[]{:S(2)}) copy-start(bf16[128,512]{1,0:T(8,128)(2,1)} %gate_ref.2) | copy-start | bytes 393220
  1.6 1.1 %copy-start.2 = (bf16[128,512]{1,0:T(8,128)(2,1)S(1)}, bf16[128,512]{1,0:T(8,128)(2,1)}, u32[]{:S(2)}) copy-start(bf16[128,512]{1,0:T(8,128)(2,1)} %v_ref.1) | copy-start | bytes 393220
  2.7 0.8 copy-start.3
  3.5 0.8 copy-start.4
  4.3 0.7 copy-start.7
  6.2 15.3 %all-to-all-start = ((bf16[4,400,128]{2,1,0:T(8,128)(2,1)}), bf16[4,400,128]{2,1,0:T(8,128)(2,1)S(1)}, u32[]{:S(2)}, u32[]{:S(2)}) async-start(bf16[4,400,128]{2,1,0:T(8,128)(2,1)} %get-tuple-element.15), calls=%async_computation | async-start | bytes 819200 | tf_op jit(solution)/shard_map/all_to_all | solution.py:271
  15.5 2.7 %collective-permute-start = (bf16[16,384]{1,0:T(8,128)(2,1)S(1)}, bf16[16,384]{1,0:T(8,128)(2,1)S(1)}, u32[]{:S(2)}, u32[]{:S(2)}) collective-permute-start(bf16[16,384]{1,0:T(8,128)(2,1)S(1)} %get-tuple-element.16), channel_id=1, source_target_pairs={{24,32},{56,64},{88,96},{120,128},{152,160},{184,192},{216,224},{2... | collective-permute-start | bytes 36872 | tf_op jit(solution)/shard_map/ppermute | solution.py:284
  16.2 2.0 %collective-permute-start.1 = (bf16[16,384]{1,0:T(8,128)(2,1)S(1)}, bf16[16,384]{1,0:T(8,128)(2,1)S(1)}, u32[]{:S(2)}, u32[]{:S(2)}) collective-permute-start(bf16[16,384]{1,0:T(8,128)(2,1)S(1)} %get-tuple-element.17), channel_id=1, source_target_pairs={{24,40},{56,72},{88,104},{120,136},{152,168},{184,200},{216,232},{... | collective-permute-start | bytes 36872 | tf_op jit(solution)/shard_map/ppermute | solution.py:284
  16.8 1.4 %collective-permute-start.2 = (bf16[16,384]{1,0:T(8,128)(2,1)S(1)}, bf16[16,384]{1,0:T(8,128)(2,1)S(1)}, u32[]{:S(2)}, u32[]{:S(2)}) collective-permute-start(bf16[16,384]{1,0:T(8,128)(2,1)S(1)} %get-tuple-element.18), channel_id=1, source_target_pairs={{24,48},{56,80},{88,112},{120,144},{152,176},{184,208},{216,240},{... | collective-permute-start | bytes 36872 | tf_op jit(solution)/shard_map/ppermute | solution.py:284
  17.5 0.7 collective-permute-start.3
  21.4 0.7 copy-start.5
  22.1 0.7 copy-start.6

commit v2 on v1

--- a/solution.py
+++ b/solution.py
@@ -58,19 +58,33 @@
     return v / (1.0 + jnp.exp(-v))
 
 
-def pack_kernel(q_ref, k_ref, v_ref, beta_ref, gate_ref, rate_ref, msg_ref, *rim_refs):
+def pack_kernel(
+    q_hbm, k_hbm, v_hbm, qk_taps_hbm, v_taps_hbm, beta_hbm, gate_hbm, rate_ref, msg_ref, taps_ref,
+    rim0, rim1, rim2, rim3, q_ref, k_ref, v_ref, qk_taps_ref, v_taps_ref, beta_ref, gate_ref, sems,
+):
+    rim_refs = (rim0, rim1, rim2, rim3)
+    sources = (beta_hbm, gate_hbm, q_hbm, k_hbm, v_hbm, qk_taps_hbm, v_taps_hbm)
+    targets = (beta_ref, gate_ref, q_ref, k_ref, v_ref, qk_taps_ref, v_taps_ref)
+    copies = [pltpu.make_async_copy(x, y, sems.at[i]) for i, (x, y) in enumerate(zip(sources, targets))]
+    for c in copies:
+        c.start()
     length = q_ref.shape[0]
-    ratio = (v_ref.shape[1] // HDIM) // (q_ref.shape[1] // HDIM)
-    beta = jax.nn.sigmoid(beta_ref[...])
-    decay = -jnp.exp(rate_ref[...]) * softplus(gate_ref[...])
-    lane = lax.broadcasted_iota(jnp.int32, (length, HDIM), 1)
-    table = jnp.zeros((length, HDIM), F32)
-    for at, values in ((0, beta), (3, decay)):
-        for p, part in enumerate(split3(values)):
-            part = part.astype(F32)
-            for h in range(GROUP):
-                table = jnp.where(lane == EXTRA * h + at + p, part[:, h : h + 1], table)
-    table = table.T
+    ratio = v_ref.shape[1] // q_ref.shape[1]
+    for c in copies[:2]:
+        c.wait()
+    beta = split3(jax.nn.sigmoid(beta_ref[...]))
+    soft = softplus(gate_ref[...])
+    head_row = lax.broadcasted_iota(jnp.int32, soft.shape, 0)
+    rate = jnp.zeros(soft.shape, F32)
+    for h in range(GROUP):
+        rate = jnp.where(head_row == h, rate_ref[h], rate)
+    decay = split3(-jnp.exp(rate) * soft)
+    blank = jnp.zeros((EXTRA - 6, length), F32)
+    for h in range(GROUP):
+        rows = [p[h : h + 1].astype(F32) for p in beta + decay] + [blank]
+        msg_ref[h, 3 * length :] = jnp.concatenate(rows, axis=0).astype(BF16)
+    for c in copies[2:]:
+        c.wait()
     for h in range(GROUP):
         kh = h // ratio
         query = q_ref[:, kh * HDIM : (kh + 1) * HDIM]
@@ -79,41 +93,35 @@
         msg_ref[h, 0:length] = query
         msg_ref[h, length : 2 * length] = keyed
         msg_ref[h, 2 * length : 3 * length] = value
-        msg_ref[h, 3 * length : 3 * length + EXTRA] = table[EXTRA * h : EXTRA * (h + 1)].astype(BF16)
         rim_refs[h][:, 0:HDIM] = query[length - 16 :]
         rim_refs[h][:, HDIM : 2 * HDIM] = keyed[length - 16 :]
         rim_refs[h][:, 2 * HDIM : 3 * HDIM] = value[length - 16 :]
-
-
-def chunk_kernel(msg_ref, rim0, rim1, rim2, rim3, qk_taps_ref, v_taps_ref, map_ref, out_ref, lift_ref):
+    place = lax.axis_index("ctx") % GROUP
+
+    def pick(taps, heads):
+        parts = [taps[:, i * HDIM : (i + 1) * HDIM] for i in heads]
+        got = parts[0]
+        for i in range(1, GROUP):
+            got = jnp.where(place == i, parts[i], got)
+        return got
+
+    key_heads = [h // ratio for h in range(GROUP)]
+    taps_ref[0:4, :] = pick(qk_taps_ref[0].astype(F32), key_heads)
+    taps_ref[4:8, :] = pick(qk_taps_ref[1].astype(F32), key_heads)
+    taps_ref[8:12, :] = pick(v_taps_ref[...].astype(F32), range(GROUP))
+    taps_ref[12:16, :] = jnp.zeros((4, HDIM), F32)
+
+
+def chunk_kernel(msg_ref, taps_ref, rim0, rim1, rim2, rim3, map_ref, out_ref, lift_ref):
     length = SPAN
     total = GROUP * length
-    place = lax.axis_index("ctx") % GROUP
     rims = [r[8:16, :].astype(F32) for r in (rim0, rim1, rim2, rim3)]
     rim = (rims[0] + rims[1]) + (rims[2] + rims[3])
-
-    def pick(parts):
-        got = parts[0]
-        for i in range(1, len(parts)):
-            got = jnp.where(place == i, parts[i], got)
-        return got
-
-    ratio = v_taps_ref.shape[1] // qk_taps_ref.shape[2]
-
-    def taps_of(ref_part, repeat):
-        heads = [ref_part[:, (h // repeat) * HDIM : (h // repeat + 1) * HDIM] for h in range(GROUP)]
-        return pick([a.astype(F32) for a in heads])
-
-    taps = (
-        taps_of(qk_taps_ref[0], ratio),
-        taps_of(qk_taps_ref[1], ratio),
-        taps_of(v_taps_ref[...], 1),
-    )
 
     def convolved(which):
         rows = [msg_ref[s, which * length : (which + 1) * length, :].astype(F32) for s in range(GROUP)]
         extended = jnp.concatenate([rim[:, which * HDIM : (which + 1) * HDIM]] + rows, axis=0)
-        tap = taps[which]
+        tap = taps_ref[4 * which : 4 * which + 4, :]
         acc = tap[CONV - 1 : CONV] * extended
         for by in range(1, CONV):
             acc = acc + tap[CONV - 1 - by : CONV - by] * pltpu.roll(extended, by, 0)
@@ -231,13 +239,18 @@
     ).astype(BF16)
 
 
-def call(body, outs, *args):
+def call(body, outs, *args, **more):
     return pl.pallas_call(
         body,
         out_shape=outs,
-        compiler_params=pltpu.CompilerParams(vmem_limit_bytes=48 * 1024 * 1024),
-        interpret=INTERPRET,
+        compiler_params=pltpu.CompilerParams(vmem_limit_bytes=32 * 1024 * 1024),
+        interpret=pltpu.InterpretParams() if INTERPRET else False,
+        **more,
     )(*args)
+
+
+def in_hbm(a):
+    return a if INTERPRET else pltpu.with_memory_space_constraint(a, pltpu.HBM)
 
 
 def local(
@@ -270,15 +283,16 @@
     def trade(a, groups):
         return lax.all_to_all(a, "ctx", 0, 0, axis_index_groups=groups)
 
-    message, *rims = call(
+    raw = (query_raw, key_raw, value_raw, query_key_conv, value_conv, beta_logit.T, gate_logit.T)
+    fetched = [pltpu.VMEM(raw[i].shape, raw[i].dtype) for i in range(len(raw))]
+    message, taps, *rims = call(
         pack_kernel,
-        [shape((GROUP, 3 * length + EXTRA, HDIM), BF16)] + [shape((16, 3 * HDIM), BF16)] * GROUP,
-        query_raw,
-        key_raw,
-        value_raw,
-        beta_logit,
-        gate_logit,
-        log_rate.reshape(1, -1),
+        [shape((GROUP, 3 * length + EXTRA, HDIM), BF16), shape((16, HDIM), F32)]
+        + [shape((16, 3 * HDIM), BF16)] * GROUP,
+        *[in_hbm(a) for a in raw],
+        in_hbm(log_rate),
+        in_specs=[pl.BlockSpec(memory_space=pltpu.HBM)] * len(raw) + [pl.BlockSpec(memory_space=pltpu.SMEM)],
+        scratch_shapes=fetched + [pltpu.SemaphoreType.DMA((len(raw),))],
     )
     rims = [
         lax.ppermute(rim, "ctx", [(i, i + 1 + h) for i in range(GROUP - 1, devices - 1, GROUP)])
@@ -293,9 +307,8 @@
             shape((GROUP * SPAN, HDIM), BF16),
         ],
         message,
+        taps,
         *rims,
-        query_key_conv,
-        value_conv,
     )
     maps = trade(maps, rows)
     totals, mine = call(

time: 91.7 us -> 86.7 us (0.945)
  local copies, waits for them, and re-layouts: 6.36 us -> 0.01 us
  Pallas kernels: 7.66 us -> 9.17 us
    unnamed x20 -> x6, local copies, waits for them, and re-layouts: 6.36 us -> 0.01 us
    pallas_call x5, Pallas kernels: 7.66 us -> 9.17 us  [call(): pl.pallas_call(body, out_shape=outs, compiler_params=pltpu.CompilerParams...]
where the time goes in v2:
time: 86.7 us; the launch traced here: 86.3 us
  blocking collectives  61.1 us (70%)
  starting transfers between devices  12 us (14%)
  Pallas kernels  9.17 us (11%)
  waiting for transfers between devices  3.25 us (4%)
    all_to_all x3, blocking collectives, trade(): return lax.all_to_all(a, 'ctx', 0, 0, axis_index_groups=groups)  36.6 us
    all_to_all x1, blocking collectives, local(): lax.all_to_all(partial.reshape(heads, length // heads, width), 'head', 0, 0)  24.5 us
    all_to_all x1, starting transfers between devices, trade(): return lax.all_to_all(a, 'ctx', 0, 0, axis_index_groups=groups)  9.35 us
    pallas_call x5, Pallas kernels, call(): pl.pallas_call(body, out_shape=outs, compiler_params=pltpu.CompilerParams...  9.17 us
    all_to_all x1, waiting for transfers between devices, trade(): return lax.all_to_all(a, 'ctx', 0, 0, axis_index_groups=groups)  3.24 us
    ppermute x4, starting transfers between devices, local(): lax.ppermute(rim, 'ctx', [(i, i + 1 + h) for i in range(GROUP - 1, device...  2.64 us
  transfers between devices with their start and end apart: 5, of which 1 were waited for; matrix products, arithmetic and copies ran while one was open for 0% of the time, Pallas kernels for 0%

profile of v2, /device:TPU:2, one launch (start us, length us, event | category | flops | bytes accessed | tf_op | source)
XLA Modules:
  0.0 86.3 jit_solution(10792071858032614003)
XLA Ops:
  0.0 0.0 copy-start.2
  0.0 0.0 copy-start
  0.0 0.0 copy-start.1
  0.0 2.7 %shard_map.109 = (bf16[4,400,128]{2,1,0:T(8,128)(2,1)}, f32[16,128]{1,0:T(8,128)S(1)}, bf16[16,384]{1,0:T(8,128)(2,1)S(1)}, bf16[16,384]{1,0:T(8,128)(2,1)S(1)},...) custom-call(bf16[128,256]{1,0:T(8,128)(2,1)} %q_hbm.1, bf16[128,256]{1,0:T(8,128)(2,1)} %k_hbm.1, ...), custom_call_target="tpu_custom_call" | custom-call | tf_op jit(solution)/shard_map/pallas_call | solution.py:243
  2.7 9.3 %all-to-all-start = ((bf16[4,400,128]{2,1,0:T(8,128)(2,1)}), bf16[4,400,128]{2,1,0:T(8,128)(2,1)S(1)}, u32[]{:S(2)}, u32[]{:S(2)}) async-start(bf16[4,400,128]{2,1,0:T(8,128)(2,1)} %get-tuple-element.16), calls=%async_computation | async-start | bytes 819200 | tf_op jit(solution)/shard_map/all_to_all | solution.py:284
  12.0 0.7 collective-permute-start
  12.7 0.7 collective-permute-start.1
  13.4 0.7 collective-permute-start.2
  14.0 0.7 collective-permute-start.3
  14.7 0.0 collective-permute-done.rim0
  14.7 0.0 collective-permute-done.1.rim1
  14.7 0.0 collective-permute-done.2.rim2
  14.7 0.0 collective-permute-done.3.rim3
  14.7 3.2 %all-to-all-done.msg_ref = bf16[4,400,128]{2,1,0:T(8,128)(2,1)S(1)} async-done(((bf16[4,400,128]{2,1,0:T(8,128)(2,1)}), bf16[4,400,128]{2,1,0:T(8,128)(2,1)S(1)}, u32[]{:S(2)}, u32[]{:S(2)}) %all-to-all-start) | async-done | bytes 409632 | tf_op jit(solution)/shard_map/all_to_all | solution.py:284
  18.0 4.6 %shard_map.110 = (bf16[4,256,128]{2,1,0:T(8,128)(2,1)S(1)}, f32[512,128]{1,0:T(8,128)S(1)}, bf16[512,128]{1,0:T(8,128)(2,1)S(1)}) custom-call(bf16[4,400,128]{2,1,0:T(8,128)(2,1)S(1)} %all-to-all-done.msg_ref, f32[16,128]{1,0:T(8,128)S(1)} %get-tuple-element.17.taps_ref, bf16[16,384]{1,0:T(8,128)(2,1)S(1)} %collective-permute-done.rim0, ...), custom_call_target="tpu_custom_call" | custom-call | tf_op jit(solution)/shard_map/pallas_call | solution.py:243
  22.6 11.4 %all_to_all.25.maps_ref = bf16[4,256,128]{2,1,0:T(8,128)(2,1)S(1)} all-to-all(bf16[4,256,128]{2,1,0:T(8,128)(2,1)S(1)} %get-tuple-element.22), channel_id=1, replica_groups={{0,32,64,96},{8,40,72,104},{16,48,80,112},{24,56,88,120},{128,160,192,2..., dimensions={0} | all-to-all | bytes 524288 | tf_op jit(solution)/shard_map/all_to_all | solution.py:284
  34.0 0.6 shard_map.111
  34.6 16.8 %all_to_all.26.totals_ref = bf16[4,256,128]{2,1,0:T(8,128)(2,1)S(1)} all-to-all(bf16[4,256,128]{2,1,0:T(8,128)(2,1)S(1)} %get-tuple-element.23), channel_id=1, replica_groups={{0,128,256,384},{8,136,264,392},{16,144,272,400},{24,152,280,408},{32,1..., dimensions={0} | all-to-all | bytes 524288 | tf_op jit(solution)/shard_map/all_to_all | solution.py:284
  51.4 0.0 copy-done.2
  51.4 0.8 shard_map.112
  52.3 8.4 %all_to_all.27.normed_ref = bf16[4,128,128]{2,1,0:T(8,128)(2,1)S(1)} all-to-all(bf16[4,128,128]{2,1,0:T(8,128)(2,1)S(1)} %shard_map.112), channel_id=1, replica_groups={{0,8,16,24},{32,40,48,56},{64,72,80,88},{96,104,112,120},{128,136,144,1..., dimensions={0} | all-to-all | bytes 262144 | tf_op jit(solution)/shard_map/all_to_all | solution.py:284
  60.6 0.0 copy-done
  60.6 0.0 copy-done.1
  60.6 0.5 shard_map.113
  61.1 24.5 %all_to_all.28 = bf16[8,16,2048]{2,1,0:T(8,128)(2,1)S(1)} all-to-all(bf16[8,16,2048]{2,1,0:T(8,128)(2,1)S(1)} %bitcast.4), channel_id=1, replica_groups=mesh['ctx'=64,'head'=8] {'head'}, dimensions={0} | all-to-all | bytes 1048576 | tf_op jit(solution)/shard_map/all_to_all | solution.py:331
  85.6 0.7 reduce_sum.12
Async XLA Ops:
  0.0 51.4 %copy-start.2 = (f32[128]{0:T(128)S(1)}, f32[128]{0:T(128)}, u32[]{:S(2)}) copy-start(f32[128]{0:T(128)} %param.20) | copy-start | bytes 1540
  0.0 60.6 %copy-start = (bf16[512,2048]{1,0:T(8,128)(2,1)S(1)}, bf16[512,2048]{1,0:T(8,128)(2,1)}, u32[]{:S(2)}) copy-start(bf16[512,2048]{1,0:T(8,128)(2,1)} %weight_ref.1) | copy-start | bytes 6291460
  0.0 60.6 %copy-start.1 = (bf16[128,512]{1,0:T(8,128)(2,1)S(1)}, bf16[128,512]{1,0:T(8,128)(2,1)}, u32[]{:S(2)}) copy-start(bf16[128,512]{1,0:T(8,128)(2,1)} %gate_ref.1) | copy-start | bytes 393220
  2.7 15.3 %all-to-all-start = ((bf16[4,400,128]{2,1,0:T(8,128)(2,1)}), bf16[4,400,128]{2,1,0:T(8,128)(2,1)S(1)}, u32[]{:S(2)}, u32[]{:S(2)}) async-start(bf16[4,400,128]{2,1,0:T(8,128)(2,1)} %get-tuple-element.16), calls=%async_computation | async-start | bytes 819200 | tf_op jit(solution)/shard_map/all_to_all | solution.py:284
  12.0 2.7 %collective-permute-start = (bf16[16,384]{1,0:T(8,128)(2,1)S(1)}, bf16[16,384]{1,0:T(8,128)(2,1)S(1)}, u32[]{:S(2)}, u32[]{:S(2)}) collective-permute-start(bf16[16,384]{1,0:T(8,128)(2,1)S(1)} %get-tuple-element.18), channel_id=1, source_target_pairs={{24,32},{56,64},{88,96},{120,128},{152,160},{184,192},{216,224},{2... | collective-permute-start | bytes 36872 | tf_op jit(solution)/shard_map/ppermute | solution.py:298
  12.7 2.0 %collective-permute-start.1 = (bf16[16,384]{1,0:T(8,128)(2,1)S(1)}, bf16[16,384]{1,0:T(8,128)(2,1)S(1)}, u32[]{:S(2)}, u32[]{:S(2)}) collective-permute-start(bf16[16,384]{1,0:T(8,128)(2,1)S(1)} %get-tuple-element.19), channel_id=1, source_target_pairs={{24,40},{56,72},{88,104},{120,136},{152,168},{184,200},{216,232},{... | collective-permute-start | bytes 36872 | tf_op jit(solution)/shard_map/ppermute | solution.py:298
  13.4 1.4 %collective-permute-start.2 = (bf16[16,384]{1,0:T(8,128)(2,1)S(1)}, bf16[16,384]{1,0:T(8,128)(2,1)S(1)}, u32[]{:S(2)}, u32[]{:S(2)}) collective-permute-start(bf16[16,384]{1,0:T(8,128)(2,1)S(1)} %get-tuple-element.20), channel_id=1, source_target_pairs={{24,48},{56,80},{88,112},{120,144},{152,176},{184,208},{216,240},{... | collective-permute-start | bytes 36872 | tf_op jit(solution)/shard_map/ppermute | solution.py:298
  14.0 0.7 collective-permute-start.3

commit v3 on v2

--- a/solution.py
+++ b/solution.py
@@ -194,7 +194,7 @@
         lift_ref[c * length : (c + 1) * length, :] = lifted.astype(BF16)
 
 
-def chain_kernel(maps_ref, total_ref, mine_ref):
+def chain_kernel(maps_ref, step_ref, add_ref, mine_ref):
     place = (lax.axis_index("ctx") // GROUP) % ROW
     row = lax.broadcasted_iota(jnp.int32, (HDIM, 2 * HDIM), 0)
     col = lax.broadcasted_iota(jnp.int32, (HDIM, 2 * HDIM), 1)
@@ -206,20 +206,20 @@
         state = jnp.concatenate(
             [moved[:, :HDIM], moved[:, HDIM:] + maps_ref[i, HDIM:, :].astype(F32)], axis=1
         )
-    for s in range(SLAB):
-        total_ref[s, :HDIM, :] = state[:, :HDIM].astype(BF16)
-        total_ref[s, HDIM:, :] = state[:, HDIM:].astype(BF16)
+    step_ref[...] = state[:, :HDIM].astype(BF16)
+    add_ref[...] = state[:, HDIM:].astype(BF16)
     mine_ref[...] = mine
 
 
-def finish_kernel(totals_ref, mine_ref, own_ref, lift_ref, gain_ref, normed_ref):
-    place = lax.axis_index("ctx") // (GROUP * ROW)
-    state = jnp.zeros((HDIM, HDIM), F32)
-    got = state
-    for i in range(1, SLAB):
-        push = totals_ref[i - 1, HDIM:, :].astype(F32)
-        state = push if i == 1 else dot_mixed(totals_ref[i - 1, :HDIM, :], state) + push
-        got = jnp.where(place == i, state, got)
+def relay_kernel(step_ref, add_ref, *refs):
+    state = refs[0][...]
+    for r in refs[1:-1]:
+        state = state + r[...]
+    refs[-1][...] = (dot1(step_ref[...], state) + add_ref[...].astype(F32)).astype(BF16)
+
+
+def finish_kernel(first_ref, second_ref, third_ref, mine_ref, own_ref, lift_ref, gain_ref, normed_ref):
+    got = first_ref[...].astype(F32) + second_ref[...].astype(F32) + third_ref[...].astype(F32)
     start = dot3(mine_ref[:, :HDIM], got) + mine_ref[:, HDIM:]
     core = own_ref[...] + dot_mixed(lift_ref[...], start)
     mean = jnp.mean(core * core, axis=-1, keepdims=True)
@@ -278,7 +278,6 @@
         for z in range(devices // reach)
         for i in range(GROUP)
     ]
-    slabs = [[z * reach + i for z in range(SLAB)] for i in range(reach)]
 
     def trade(a, groups):
         return lax.all_to_all(a, "ctx", 0, 0, axis_index_groups=groups)
@@ -311,16 +310,17 @@
         *rims,
     )
     maps = trade(maps, rows)
-    totals, mine = call(
-        chain_kernel,
-        [shape((SLAB, 2 * HDIM, HDIM), BF16), shape((HDIM, 2 * HDIM), F32)],
-        maps,
-    )
-    totals = trade(totals, slabs)
+    block = shape((HDIM, HDIM), BF16)
+    step, add, mine = call(chain_kernel, [block, block, shape((HDIM, 2 * HDIM), F32)], maps)
+    states = []
+    for slab in range(SLAB - 1):
+        leaving = call(relay_kernel, block, step, add, *states) if slab else add
+        pairs = [(reach * slab + i, reach * (slab + 1) + i) for i in range(reach)]
+        states.append(lax.ppermute(leaving, "ctx", pairs))
     normed = call(
         finish_kernel,
         shape((GROUP, SPAN, HDIM), BF16),
-        totals,
+        *states,
         mine,
         own,
         lifted,

time: 86.7 us -> 79 us (0.911)
  the two profiles are of different devices: /device:TPU:2 before, /device:TPU:384 now
where the time goes in v3:
time: 79 us; the launch traced here: 78.6 us
  blocking collectives  44.5 us (56%)
  waiting for transfers between devices  14.8 us (19%)
  starting transfers between devices  9.36 us (12%)
  Pallas kernels  9.12 us (12%)
    all_to_all x1, blocking collectives, local(): lax.all_to_all(partial.reshape(heads, length // heads, width), 'head', 0, 0)  24 us
    all_to_all x2, blocking collectives, trade(): return lax.all_to_all(a, 'ctx', 0, 0, axis_index_groups=groups)  20.5 us
    ppermute x3, waiting for transfers between devices, local(): states.append(lax.ppermute(leaving, 'ctx', pairs))  10.6 us
    pallas_call x7, Pallas kernels, call(): pl.pallas_call(body, out_shape=outs, compiler_params=pltpu.CompilerParams...  9.12 us
    ppermute x4, waiting for transfers between devices, local(): lax.ppermute(rim, 'ctx', [(i, i + 1 + h) for i in range(GROUP - 1, device...  3.82 us
    all_to_all x1, starting transfers between devices, trade(): return lax.all_to_all(a, 'ctx', 0, 0, axis_index_groups=groups)  3.47 us
    ppermute x4, starting transfers between devices, local(): lax.ppermute(rim, 'ctx', [(i, i + 1 + h) for i in range(GROUP - 1, device...  3.28 us
    ppermute x3, starting transfers between devices, local(): states.append(lax.ppermute(leaving, 'ctx', pairs))  2.61 us
  transfers between devices with their start and end apart: 8, of which 3 were waited for; matrix products, arithmetic and copies ran while one was open for 0% of the time, Pallas kernels for 0%

profile of v3, /device:TPU:384, one launch (start us, length us, event | category | flops | bytes accessed | tf_op | source)
XLA Modules:
  0.0 78.6 jit_solution(6003271011177824574)
XLA Ops:
  0.0 0.0 copy-start.2
  0.0 0.0 copy-start
  0.0 0.0 copy-start.1
  0.0 2.7 %shard_map.109 = (bf16[4,400,128]{2,1,0:T(8,128)(2,1)}, f32[16,128]{1,0:T(8,128)S(1)}, bf16[16,384]{1,0:T(8,128)(2,1)S(1)}, bf16[16,384]{1,0:T(8,128)(2,1)S(1)},...) custom-call(bf16[128,256]{1,0:T(8,128)(2,1)} %q_hbm.1, bf16[128,256]{1,0:T(8,128)(2,1)} %k_hbm.1, ...), custom_call_target="tpu_custom_call" | custom-call | tf_op jit(solution)/shard_map/pallas_call | solution.py:243
  2.7 3.5 %all-to-all-start = ((bf16[4,400,128]{2,1,0:T(8,128)(2,1)}), bf16[4,400,128]{2,1,0:T(8,128)(2,1)S(1)}, u32[]{:S(2)}, u32[]{:S(2)}) async-start(bf16[4,400,128]{2,1,0:T(8,128)(2,1)} %get-tuple-element.17), calls=%async_computation | async-start | bytes 819200 | tf_op jit(solution)/shard_map/all_to_all | solution.py:283
  6.2 1.3 %collective-permute-start = (bf16[16,384]{1,0:T(8,128)(2,1)S(1)}, bf16[16,384]{1,0:T(8,128)(2,1)S(1)}, u32[]{:S(2)}, u32[]{:S(2)}) collective-permute-start(bf16[16,384]{1,0:T(8,128)(2,1)S(1)} %get-tuple-element.19), channel_id=1, source_target_pairs={{24,32},{56,64},{88,96},{120,128},{152,160},{184,192},{216,224},{2... | collective-permute-start | bytes 36872 | tf_op jit(solution)/shard_map/ppermute | solution.py:297
  7.5 0.7 collective-permute-start.1
  8.1 0.7 collective-permute-start.2
  8.8 0.7 collective-permute-start.3
  9.5 3.8 %collective-permute-done.rim0 = bf16[16,384]{1,0:T(8,128)(2,1)S(1)} collective-permute-done((bf16[16,384]{1,0:T(8,128)(2,1)S(1)}, bf16[16,384]{1,0:T(8,128)(2,1)S(1)}, u32[]{:S(2)}, u32[]{:S(2)}) %collective-permute-start) | collective-permute-done | bytes 12320 | tf_op jit(solution)/shard_map/ppermute | solution.py:297
  13.3 0.0 collective-permute-done.1.rim1
  13.3 0.0 collective-permute-done.2.rim2
  13.3 0.0 collective-permute-done.3.rim3
  13.3 0.4 all-to-all-done.msg_ref
  13.8 4.6 %shard_map.110 = (bf16[4,256,128]{2,1,0:T(8,128)(2,1)S(1)}, f32[512,128]{1,0:T(8,128)S(1)}, bf16[512,128]{1,0:T(8,128)(2,1)S(1)}) custom-call(bf16[4,400,128]{2,1,0:T(8,128)(2,1)S(1)} %all-to-all-done.msg_ref, f32[16,128]{1,0:T(8,128)S(1)} %get-tuple-element.18.taps_ref, bf16[16,384]{1,0:T(8,128)(2,1)S(1)} %collective-permute-done.rim0, ...), custom_call_target="tpu_custom_call" | custom-call | tf_op jit(solution)/shard_map/pallas_call | solution.py:243
  18.4 12.2 %all_to_all.20.maps_ref = bf16[4,256,128]{2,1,0:T(8,128)(2,1)S(1)} all-to-all(bf16[4,256,128]{2,1,0:T(8,128)(2,1)S(1)} %get-tuple-element.23), channel_id=1, replica_groups={{0,32,64,96},{8,40,72,104},{16,48,80,112},{24,56,88,120},{128,160,192,2..., dimensions={0} | all-to-all | bytes 524288 | tf_op jit(solution)/shard_map/all_to_all | solution.py:283
  30.6 0.6 shard_map.111
  31.2 0.7 collective-permute-start.4
  31.9 0.0 collective-permute-done.4.refs_0_.first_ref
  31.9 0.1 shard_map.112
  32.0 0.7 collective-permute-start.5
  32.7 0.0 collective-permute-done.5.refs_1_.second_ref
  32.7 0.1 shard_map.113
  32.8 1.3 %collective-permute-start.6 = (bf16[128,128]{1,0:T(8,128)(2,1)S(1)}, bf16[128,128]{1,0:T(8,128)(2,1)S(1)}, u32[]{:S(2)}, u32[]{:S(2)}) collective-permute-start(bf16[128,128]{1,0:T(8,128)(2,1)S(1)} %shard_map.113), channel_id=1, source_target_pairs={{256,384},{264,392},{272,400},{280,408},{288,416},{296,424},{304,4... | collective-permute-start | bytes 98312 | tf_op jit(solution)/shard_map/ppermute | solution.py:319
  34.1 10.6 %collective-permute-done.6.third_ref = bf16[128,128]{1,0:T(8,128)(2,1)S(1)} collective-permute-done((bf16[128,128]{1,0:T(8,128)(2,1)S(1)}, bf16[128,128]{1,0:T(8,128)(2,1)S(1)}, u32[]{:S(2)}, u32[]{:S(2)}) %collective-permute-start.6) | collective-permute-done | bytes 32800 | tf_op jit(solution)/shard_map/ppermute | solution.py:319
  44.7 0.0 copy-done.2
  44.7 0.5 shard_map.114
  45.2 8.2 %all_to_all.21.normed_ref = bf16[4,128,128]{2,1,0:T(8,128)(2,1)S(1)} all-to-all(bf16[4,128,128]{2,1,0:T(8,128)(2,1)S(1)} %shard_map.114), channel_id=1, replica_groups={{0,8,16,24},{32,40,48,56},{64,72,80,88},{96,104,112,120},{128,136,144,1..., dimensions={0} | all-to-all | bytes 262144 | tf_op jit(solution)/shard_map/all_to_all | solution.py:283
  53.4 0.0 copy-done
  53.4 0.0 copy-done.1
  53.4 0.5 shard_map.115
  53.9 24.0 %all_to_all.22 = bf16[8,16,2048]{2,1,0:T(8,128)(2,1)S(1)} all-to-all(bf16[8,16,2048]{2,1,0:T(8,128)(2,1)S(1)} %bitcast.4), channel_id=1, replica_groups=mesh['ctx'=64,'head'=8] {'head'}, dimensions={0} | all-to-all | bytes 1048576 | tf_op jit(solution)/shard_map/all_to_all | solution.py:331
  77.9 0.7 reduce_sum.12
Async XLA Ops:
  0.0 44.7 %copy-start.2 = (f32[128]{0:T(128)S(1)}, f32[128]{0:T(128)}, u32[]{:S(2)}) copy-start(f32[128]{0:T(128)} %param.20) | copy-start | bytes 1540
  0.0 53.4 %copy-start = (bf16[512,2048]{1,0:T(8,128)(2,1)S(1)}, bf16[512,2048]{1,0:T(8,128)(2,1)}, u32[]{:S(2)}) copy-start(bf16[512,2048]{1,0:T(8,128)(2,1)} %weight_ref.1) | copy-start | bytes 6291460
  0.0 53.4 %copy-start.1 = (bf16[128,512]{1,0:T(8,128)(2,1)S(1)}, bf16[128,512]{1,0:T(8,128)(2,1)}, u32[]{:S(2)}) copy-start(bf16[128,512]{1,0:T(8,128)(2,1)} %gate_ref.1) | copy-start | bytes 393220
  2.7 11.1 %all-to-all-start = ((bf16[4,400,128]{2,1,0:T(8,128)(2,1)}), bf16[4,400,128]{2,1,0:T(8,128)(2,1)S(1)}, u32[]{:S(2)}, u32[]{:S(2)}) async-start(bf16[4,400,128]{2,1,0:T(8,128)(2,1)} %get-tuple-element.17), calls=%async_computation | async-start | bytes 819200 | tf_op jit(solution)/shard_map/all_to_all | solution.py:283
  6.2 7.1 %collective-permute-start = (bf16[16,384]{1,0:T(8,128)(2,1)S(1)}, bf16[16,384]{1,0:T(8,128)(2,1)S(1)}, u32[]{:S(2)}, u32[]{:S(2)}) collective-permute-start(bf16[16,384]{1,0:T(8,128)(2,1)S(1)} %get-tuple-element.19), channel_id=1, source_target_pairs={{24,32},{56,64},{88,96},{120,128},{152,160},{184,192},{216,224},{2... | collective-permute-start | bytes 36872 | tf_op jit(solution)/shard_map/ppermute | solution.py:297
  7.5 5.8 %collective-permute-start.1 = (bf16[16,384]{1,0:T(8,128)(2,1)S(1)}, bf16[16,384]{1,0:T(8,128)(2,1)S(1)}, u32[]{:S(2)}, u32[]{:S(2)}) collective-permute-start(bf16[16,384]{1,0:T(8,128)(2,1)S(1)} %get-tuple-element.20), channel_id=1, source_target_pairs={{24,40},{56,72},{88,104},{120,136},{152,168},{184,200},{216,232},{... | collective-permute-start | bytes 36872 | tf_op jit(solution)/shard_map/ppermute | solution.py:297
  8.1 5.2 %collective-permute-start.2 = (bf16[16,384]{1,0:T(8,128)(2,1)S(1)}, bf16[16,384]{1,0:T(8,128)(2,1)S(1)}, u32[]{:S(2)}, u32[]{:S(2)}) collective-permute-start(bf16[16,384]{1,0:T(8,128)(2,1)S(1)} %get-tuple-element.21), channel_id=1, source_target_pairs={{24,48},{56,80},{88,112},{120,144},{152,176},{184,208},{216,240},{... | collective-permute-start | bytes 36872 | tf_op jit(solution)/shard_map/ppermute | solution.py:297
  8.8 4.5 %collective-permute-start.3 = (bf16[16,384]{1,0:T(8,128)(2,1)S(1)}, bf16[16,384]{1,0:T(8,128)(2,1)S(1)}, u32[]{:S(2)}, u32[]{:S(2)}) collective-permute-start(bf16[16,384]{1,0:T(8,128)(2,1)S(1)} %get-tuple-element.22), channel_id=1, source_target_pairs={{24,56},{56,88},{88,120},{120,152},{152,184},{184,216},{216,248},{... | collective-permute-start | bytes 36872 | tf_op jit(solution)/shard_map/ppermute | solution.py:297
  31.2 0.7 collective-permute-start.4
  32.0 0.7 collective-permute-start.5
  32.8 11.9 %collective-permute-start.6 = (bf16[128,128]{1,0:T(8,128)(2,1)S(1)}, bf16[128,128]{1,0:T(8,128)(2,1)S(1)}, u32[]{:S(2)}, u32[]{:S(2)}) collective-permute-start(bf16[128,128]{1,0:T(8,128)(2,1)S(1)} %shard_map.113), channel_id=1, source_target_pairs={{256,384},{264,392},{272,400},{280,408},{288,416},{296,424},{304,4... | collective-permute-start | bytes 98312 | tf_op jit(solution)/shard_map/ppermute | solution.py:319

commit v4 on v3

--- a/solution.py
+++ b/solution.py
@@ -151,7 +151,7 @@
     gamma_col = [e[:, 3:4] + e[:, 4:5] + e[:, 5:6] for e in run_col]
     gamma_end = [g[length - 1 :] for g in gamma_col]
     within = [
-        jnp.where(row >= col, jnp.exp(jnp.where(row >= col, gamma_col[c] - gamma_row[c], 0.0)), 0.0)
+        jnp.where(row >= col, jnp.exp(jnp.where(row >= col, jnp.minimum(gamma_col[c] - gamma_row[c], 0.0), 0.0)), 0.0)
         * beta_row[c]
         for c in chunks
     ]
@@ -168,7 +168,7 @@
         size *= 2
     right = [jnp.concatenate([grow[c] * keys[c], at(value, c)], axis=1) for c in chunks]
     solved = [dot3(inverse[c], right[c]) for c in chunks]
-    tail = [(jnp.exp(gamma_end[c] - gamma_col[c]) * beta_col[c]) * keys[c] for c in chunks]
+    tail = [(jnp.exp(jnp.minimum(gamma_end[c] - gamma_col[c], 0.0)) * beta_col[c]) * keys[c] for c in chunks]
     pushed = [dot3(tail[c], solved[c], TN) for c in chunks]
     steps = [jnp.exp(gamma_end[c]) * eye - pushed[c][:, :HDIM] for c in chunks]
     adds = [pushed[c][:, HDIM:] for c in chunks]
@@ -298,6 +298,7 @@
         for h, rim in enumerate(rims)
     ]
     message = trade(message, near)
+    message, out_weight, output_gate = lax.optimization_barrier((message, out_weight, output_gate))
     maps, own, lifted = call(
         chunk_kernel,
         [

time: 79 us -> 79 us (level)
    all_to_all x1, waiting for transfers between devices: 0.45 us -> 4.27 us  [trade(): return lax.all_to_all(a, 'ctx', 0, 0, axis_index_groups=groups)]
    ppermute x4, waiting for transfers between devices: 3.82 us -> 0.01 us  [local(): lax.ppermute(rim, 'ctx', [(i, i + 1 + h) for i in range(GROUP - 1, device...]
  transfers between devices with their start and end apart: 8 -> 8, of which waited for: 3 -> 2; matrix products, arithmetic and copies ran while one was open for 0% -> 0% of each run, Pallas kernels for 0% -> 0%
where the time goes in v4:
time: 79 us; the launch traced here: 78.6 us
  blocking collectives  44.5 us (56%)
  waiting for transfers between devices  14.9 us (19%)
  starting transfers between devices  9.36 us (12%)
  Pallas kernels  9.09 us (12%)
    all_to_all x1, blocking collectives, local(): lax.all_to_all(partial.reshape(heads, length // heads, width), 'head', 0, 0)  24 us
    all_to_all x2, blocking collectives, trade(): return lax.all_to_all(a, 'ctx', 0, 0, axis_index_groups=groups)  20.4 us
    ppermute x3, waiting for transfers between devices, local(): states.append(lax.ppermute(leaving, 'ctx', pairs))  10.6 us
    pallas_call x7, Pallas kernels, call(): pl.pallas_call(body, out_shape=outs, compiler_params=pltpu.CompilerParams...  9.09 us
    all_to_all x1, waiting for transfers between devices, trade(): return lax.all_to_all(a, 'ctx', 0, 0, axis_index_groups=groups)  4.27 us
    all_to_all x1, starting transfers between devices, trade(): return lax.all_to_all(a, 'ctx', 0, 0, axis_index_groups=groups)  3.47 us
    ppermute x4, starting transfers between devices, local(): lax.ppermute(rim, 'ctx', [(i, i + 1 + h) for i in range(GROUP - 1, device...  3.28 us
    ppermute x3, starting transfers between devices, local(): states.append(lax.ppermute(leaving, 'ctx', pairs))  2.61 us
  transfers between devices with their start and end apart: 8, of which 2 were waited for; matrix products, arithmetic and copies ran while one was open for 0% of the time, Pallas kernels for 0%

profile of v4, /device:TPU:384, one launch (start us, length us, event | category | flops | bytes accessed | tf_op | source)
XLA Modules:
  0.0 78.6 jit_solution(7301467284121975161)
XLA Ops:
  0.0 0.0 copy-start
  0.0 0.0 copy-start.1
  0.0 0.0 copy-start.2
  0.0 2.7 %shard_map.109 = (bf16[4,400,128]{2,1,0:T(8,128)(2,1)}, f32[16,128]{1,0:T(8,128)S(1)}, bf16[16,384]{1,0:T(8,128)(2,1)S(1)}, bf16[16,384]{1,0:T(8,128)(2,1)S(1)},...) custom-call(bf16[128,256]{1,0:T(8,128)(2,1)} %q_hbm.1, bf16[128,256]{1,0:T(8,128)(2,1)} %k_hbm.1, ...), custom_call_target="tpu_custom_call" | custom-call | tf_op jit(solution)/shard_map/pallas_call | solution.py:243
  2.7 3.5 %all-to-all-start = ((bf16[4,400,128]{2,1,0:T(8,128)(2,1)}), bf16[4,400,128]{2,1,0:T(8,128)(2,1)S(1)}, u32[]{:S(2)}, u32[]{:S(2)}) async-start(bf16[4,400,128]{2,1,0:T(8,128)(2,1)} %get-tuple-element.20), calls=%async_computation | async-start | bytes 819200 | tf_op jit(solution)/shard_map/all_to_all | solution.py:283
  6.2 1.3 %collective-permute-start = (bf16[16,384]{1,0:T(8,128)(2,1)S(1)}, bf16[16,384]{1,0:T(8,128)(2,1)S(1)}, u32[]{:S(2)}, u32[]{:S(2)}) collective-permute-start(bf16[16,384]{1,0:T(8,128)(2,1)S(1)} %get-tuple-element.23), channel_id=1, source_target_pairs={{24,32},{56,64},{88,96},{120,128},{152,160},{184,192},{216,224},{2... | collective-permute-start | bytes 36872 | tf_op jit(solution)/shard_map/ppermute | solution.py:297
  7.5 0.7 collective-permute-start.1
  8.1 0.7 collective-permute-start.2
  8.8 0.7 collective-permute-start.3
  9.5 4.3 %all-to-all-done.msg_ref = bf16[4,400,128]{2,1,0:T(8,128)(2,1)S(1)} async-done(((bf16[4,400,128]{2,1,0:T(8,128)(2,1)}), bf16[4,400,128]{2,1,0:T(8,128)(2,1)S(1)}, u32[]{:S(2)}, u32[]{:S(2)}) %all-to-all-start) | async-done | bytes 409632 | tf_op jit(solution)/shard_map/all_to_all | solution.py:283
  13.8 0.0 collective-permute-done.rim0
  13.8 0.0 collective-permute-done.1.rim1
  13.8 0.0 collective-permute-done.2.rim2
  13.8 0.0 collective-permute-done.3.rim3
  13.8 4.6 %shard_map.110 = (bf16[4,256,128]{2,1,0:T(8,128)(2,1)S(1)}, f32[512,128]{1,0:T(8,128)S(1)}, bf16[512,128]{1,0:T(8,128)(2,1)S(1)}) custom-call(bf16[4,400,128]{2,1,0:T(8,128)(2,1)S(1)} %all-to-all-done.msg_ref, f32[16,128]{1,0:T(8,128)S(1)} %get-tuple-element.22.taps_ref, bf16[16,384]{1,0:T(8,128)(2,1)S(1)} %collective-permute-done.rim0, ...), custom_call_target="tpu_custom_call" | custom-call | tf_op jit(solution)/shard_map/pallas_call | solution.py:243
  18.4 12.2 %all_to_all.20.maps_ref = bf16[4,256,128]{2,1,0:T(8,128)(2,1)S(1)} all-to-all(bf16[4,256,128]{2,1,0:T(8,128)(2,1)S(1)} %get-tuple-element.27), channel_id=1, replica_groups={{0,32,64,96},{8,40,72,104},{16,48,80,112},{24,56,88,120},{128,160,192,2..., dimensions={0} | all-to-all | bytes 524288 | tf_op jit(solution)/shard_map/all_to_all | solution.py:283
  30.6 0.5 shard_map.111
  31.2 0.7 collective-permute-start.4
  31.9 0.0 collective-permute-done.4.refs_0_.first_ref
  31.9 0.1 shard_map.112
  32.0 0.7 collective-permute-start.5
  32.7 0.0 collective-permute-done.5.refs_1_.second_ref
  32.7 0.1 shard_map.113
  32.8 1.3 %collective-permute-start.6 = (bf16[128,128]{1,0:T(8,128)(2,1)S(1)}, bf16[128,128]{1,0:T(8,128)(2,1)S(1)}, u32[]{:S(2)}, u32[]{:S(2)}) collective-permute-start(bf16[128,128]{1,0:T(8,128)(2,1)S(1)} %shard_map.113), channel_id=1, source_target_pairs={{256,384},{264,392},{272,400},{280,408},{288,416},{296,424},{304,4... | collective-permute-start | bytes 98312 | tf_op jit(solution)/shard_map/ppermute | solution.py:320
  34.1 10.6 %collective-permute-done.6.third_ref = bf16[128,128]{1,0:T(8,128)(2,1)S(1)} collective-permute-done((bf16[128,128]{1,0:T(8,128)(2,1)S(1)}, bf16[128,128]{1,0:T(8,128)(2,1)S(1)}, u32[]{:S(2)}, u32[]{:S(2)}) %collective-permute-start.6) | collective-permute-done | bytes 32800 | tf_op jit(solution)/shard_map/ppermute | solution.py:320
  44.7 0.0 copy-done.2
  44.7 0.5 shard_map.114
  45.2 8.2 %all_to_all.21.normed_ref = bf16[4,128,128]{2,1,0:T(8,128)(2,1)S(1)} all-to-all(bf16[4,128,128]{2,1,0:T(8,128)(2,1)S(1)} %shard_map.114), channel_id=1, replica_groups={{0,8,16,24},{32,40,48,56},{64,72,80,88},{96,104,112,120},{128,136,144,1..., dimensions={0} | all-to-all | bytes 262144 | tf_op jit(solution)/shard_map/all_to_all | solution.py:283
  53.4 0.0 copy-done
  53.4 0.0 copy-done.1
  53.4 0.5 shard_map.115
  53.9 24.0 %all_to_all.22 = bf16[8,16,2048]{2,1,0:T(8,128)(2,1)S(1)} all-to-all(bf16[8,16,2048]{2,1,0:T(8,128)(2,1)S(1)} %bitcast.4), channel_id=1, replica_groups=mesh['ctx'=64,'head'=8] {'head'}, dimensions={0} | all-to-all | bytes 1048576 | tf_op jit(solution)/shard_map/all_to_all | solution.py:332
  77.9 0.7 reduce_sum.12
Async XLA Ops:
  0.0 53.4 %copy-start = (bf16[512,2048]{1,0:T(8,128)(2,1)S(1)}, bf16[512,2048]{1,0:T(8,128)(2,1)}, u32[]{:S(2)}) copy-start(bf16[512,2048]{1,0:T(8,128)(2,1)} %weight_ref) | copy-start | bytes 6291460
  0.0 53.4 %copy-start.1 = (bf16[128,512]{1,0:T(8,128)(2,1)S(1)}, bf16[128,512]{1,0:T(8,128)(2,1)}, u32[]{:S(2)}) copy-start(bf16[128,512]{1,0:T(8,128)(2,1)} %gate_ref) | copy-start | bytes 393220
  0.0 44.7 %copy-start.2 = (f32[128]{0:T(128)S(1)}, f32[128]{0:T(128)}, u32[]{:S(2)}) copy-start(f32[128]{0:T(128)} %param.20) | copy-start | bytes 1540
  2.7 11.1 %all-to-all-start = ((bf16[4,400,128]{2,1,0:T(8,128)(2,1)}), bf16[4,400,128]{2,1,0:T(8,128)(2,1)S(1)}, u32[]{:S(2)}, u32[]{:S(2)}) async-start(bf16[4,400,128]{2,1,0:T(8,128)(2,1)} %get-tuple-element.20), calls=%async_computation | async-start | bytes 819200 | tf_op jit(solution)/shard_map/all_to_all | solution.py:283
  6.2 7.6 %collective-permute-start = (bf16[16,384]{1,0:T(8,128)(2,1)S(1)}, bf16[16,384]{1,0:T(8,128)(2,1)S(1)}, u32[]{:S(2)}, u32[]{:S(2)}) collective-permute-start(bf16[16,384]{1,0:T(8,128)(2,1)S(1)} %get-tuple-element.23), channel_id=1, source_target_pairs={{24,32},{56,64},{88,96},{120,128},{152,160},{184,192},{216,224},{2... | collective-permute-start | bytes 36872 | tf_op jit(solution)/shard_map/ppermute | solution.py:297
  7.5 6.3 %collective-permute-start.1 = (bf16[16,384]{1,0:T(8,128)(2,1)S(1)}, bf16[16,384]{1,0:T(8,128)(2,1)S(1)}, u32[]{:S(2)}, u32[]{:S(2)}) collective-permute-start(bf16[16,384]{1,0:T(8,128)(2,1)S(1)} %get-tuple-element.24), channel_id=1, source_target_pairs={{24,40},{56,72},{88,104},{120,136},{152,168},{184,200},{216,232},{... | collective-permute-start | bytes 36872 | tf_op jit(solution)/shard_map/ppermute | solution.py:297
  8.1 5.6 %collective-permute-start.2 = (bf16[16,384]{1,0:T(8,128)(2,1)S(1)}, bf16[16,384]{1,0:T(8,128)(2,1)S(1)}, u32[]{:S(2)}, u32[]{:S(2)}) collective-permute-start(bf16[16,384]{1,0:T(8,128)(2,1)S(1)} %get-tuple-element.25), channel_id=1, source_target_pairs={{24,48},{56,80},{88,112},{120,144},{152,176},{184,208},{216,240},{... | collective-permute-start | bytes 36872 | tf_op jit(solution)/shard_map/ppermute | solution.py:297
  8.8 5.0 %collective-permute-start.3 = (bf16[16,384]{1,0:T(8,128)(2,1)S(1)}, bf16[16,384]{1,0:T(8,128)(2,1)S(1)}, u32[]{:S(2)}, u32[]{:S(2)}) collective-permute-start(bf16[16,384]{1,0:T(8,128)(2,1)S(1)} %get-tuple-element.26), channel_id=1, source_target_pairs={{24,56},{56,88},{88,120},{120,152},{152,184},{184,216},{216,248},{... | collective-permute-start | bytes 36872 | tf_op jit(solution)/shard_map/ppermute | solution.py:297
  31.2 0.7 collective-permute-start.4
  32.0 0.7 collective-permute-start.5
  32.8 11.9 %collective-permute-start.6 = (bf16[128,128]{1,0:T(8,128)(2,1)S(1)}, bf16[128,128]{1,0:T(8,128)(2,1)S(1)}, u32[]{:S(2)}, u32[]{:S(2)}) collective-permute-start(bf16[128,128]{1,0:T(8,128)(2,1)S(1)} %shard_map.113), channel_id=1, source_target_pairs={{256,384},{264,392},{272,400},{280,408},{288,416},{296,424},{304,4... | collective-permute-start | bytes 98312 | tf_op jit(solution)/shard_map/ppermute | solution.py:320

commit v5 on v4

--- a/solution.py
+++ b/solution.py
@@ -220,7 +220,8 @@
 
 def finish_kernel(first_ref, second_ref, third_ref, mine_ref, own_ref, lift_ref, gain_ref, normed_ref):
     got = first_ref[...].astype(F32) + second_ref[...].astype(F32) + third_ref[...].astype(F32)
-    start = dot3(mine_ref[:, :HDIM], got) + mine_ref[:, HDIM:]
+    high, low = split2(mine_ref[:, :HDIM])
+    start = dot1(high, got) + dot1(low, got) + mine_ref[:, HDIM:]
     core = own_ref[...] + dot_mixed(lift_ref[...], start)
     mean = jnp.mean(core * core, axis=-1, keepdims=True)
     normed = (core * lax.rsqrt(mean + 1e-06) * gain_ref[...]).astype(BF16)

time: 79 us -> 79 us (level)
  no operation moved by 1% of the time
where the time goes in v5:
time: 79 us; the launch traced here: 78.6 us
  blocking collectives  44.5 us (56%)
  waiting for transfers between devices  14.9 us (19%)
  starting transfers between devices  9.36 us (12%)
  Pallas kernels  9.07 us (11%)
    all_to_all x1, blocking collectives, local(): lax.all_to_all(partial.reshape(heads, length // heads, width), 'head', 0, 0)  24 us
    all_to_all x2, blocking collectives, trade(): return lax.all_to_all(a, 'ctx', 0, 0, axis_index_groups=groups)  20.4 us
    ppermute x3, waiting for transfers between devices, local(): states.append(lax.ppermute(leaving, 'ctx', pairs))  10.6 us
    pallas_call x7, Pallas kernels, call(): pl.pallas_call(body, out_shape=outs, compiler_params=pltpu.CompilerParams...  9.07 us
    all_to_all x1, waiting for transfers between devices, trade(): return lax.all_to_all(a, 'ctx', 0, 0, axis_index_groups=groups)  4.27 us
    all_to_all x1, starting transfers between devices, trade(): return lax.all_to_all(a, 'ctx', 0, 0, axis_index_groups=groups)  3.47 us
    ppermute x4, starting transfers between devices, local(): lax.ppermute(rim, 'ctx', [(i, i + 1 + h) for i in range(GROUP - 1, device...  3.28 us
    ppermute x3, starting transfers between devices, local(): states.append(lax.ppermute(leaving, 'ctx', pairs))  2.61 us
  transfers between devices with their start and end apart: 8, of which 2 were waited for; matrix products, arithmetic and copies ran while one was open for 0% of the time, Pallas kernels for 0%

profile of v5, /device:TPU:384, one launch (start us, length us, event | category | flops | bytes accessed | tf_op | source)
XLA Modules:
  0.0 78.6 jit_solution(4800263067758893182)
XLA Ops:
  0.0 0.0 copy-start
  0.0 0.0 copy-start.1
  0.0 0.0 copy-start.2
  0.0 2.7 %shard_map.109 = (bf16[4,400,128]{2,1,0:T(8,128)(2,1)}, f32[16,128]{1,0:T(8,128)S(1)}, bf16[16,384]{1,0:T(8,128)(2,1)S(1)}, bf16[16,384]{1,0:T(8,128)(2,1)S(1)},...) custom-call(bf16[128,256]{1,0:T(8,128)(2,1)} %q_hbm.1, bf16[128,256]{1,0:T(8,128)(2,1)} %k_hbm.1, ...), custom_call_target="tpu_custom_call" | custom-call | tf_op jit(solution)/shard_map/pallas_call | solution.py:244
  2.7 3.5 %all-to-all-start = ((bf16[4,400,128]{2,1,0:T(8,128)(2,1)}), bf16[4,400,128]{2,1,0:T(8,128)(2,1)S(1)}, u32[]{:S(2)}, u32[]{:S(2)}) async-start(bf16[4,400,128]{2,1,0:T(8,128)(2,1)} %get-tuple-element.20), calls=%async_computation | async-start | bytes 819200 | tf_op jit(solution)/shard_map/all_to_all | solution.py:284
  6.2 1.3 %collective-permute-start = (bf16[16,384]{1,0:T(8,128)(2,1)S(1)}, bf16[16,384]{1,0:T(8,128)(2,1)S(1)}, u32[]{:S(2)}, u32[]{:S(2)}) collective-permute-start(bf16[16,384]{1,0:T(8,128)(2,1)S(1)} %get-tuple-element.23), channel_id=1, source_target_pairs={{24,32},{56,64},{88,96},{120,128},{152,160},{184,192},{216,224},{2... | collective-permute-start | bytes 36872 | tf_op jit(solution)/shard_map/ppermute | solution.py:298
  7.5 0.7 collective-permute-start.1
  8.1 0.7 collective-permute-start.2
  8.8 0.7 collective-permute-start.3
  9.5 4.3 %all-to-all-done.msg_ref = bf16[4,400,128]{2,1,0:T(8,128)(2,1)S(1)} async-done(((bf16[4,400,128]{2,1,0:T(8,128)(2,1)}), bf16[4,400,128]{2,1,0:T(8,128)(2,1)S(1)}, u32[]{:S(2)}, u32[]{:S(2)}) %all-to-all-start) | async-done | bytes 409632 | tf_op jit(solution)/shard_map/all_to_all | solution.py:284
  13.8 0.0 collective-permute-done.rim0
  13.8 0.0 collective-permute-done.1.rim1
  13.8 0.0 collective-permute-done.2.rim2
  13.8 0.0 collective-permute-done.3.rim3
  13.8 4.6 %shard_map.110 = (bf16[4,256,128]{2,1,0:T(8,128)(2,1)S(1)}, f32[512,128]{1,0:T(8,128)S(1)}, bf16[512,128]{1,0:T(8,128)(2,1)S(1)}) custom-call(bf16[4,400,128]{2,1,0:T(8,128)(2,1)S(1)} %all-to-all-done.msg_ref, f32[16,128]{1,0:T(8,128)S(1)} %get-tuple-element.22.taps_ref, bf16[16,384]{1,0:T(8,128)(2,1)S(1)} %collective-permute-done.rim0, ...), custom_call_target="tpu_custom_call" | custom-call | tf_op jit(solution)/shard_map/pallas_call | solution.py:244
  18.4 12.2 %all_to_all.20.maps_ref = bf16[4,256,128]{2,1,0:T(8,128)(2,1)S(1)} all-to-all(bf16[4,256,128]{2,1,0:T(8,128)(2,1)S(1)} %get-tuple-element.27), channel_id=1, replica_groups={{0,32,64,96},{8,40,72,104},{16,48,80,112},{24,56,88,120},{128,160,192,2..., dimensions={0} | all-to-all | bytes 524288 | tf_op jit(solution)/shard_map/all_to_all | solution.py:284
  30.6 0.5 shard_map.111
  31.2 0.7 collective-permute-start.4
  31.9 0.0 collective-permute-done.4.refs_0_.first_ref
  31.9 0.1 shard_map.112
  32.0 0.7 collective-permute-start.5
  32.7 0.0 collective-permute-done.5.refs_1_.second_ref
  32.7 0.1 shard_map.113
  32.8 1.3 %collective-permute-start.6 = (bf16[128,128]{1,0:T(8,128)(2,1)S(1)}, bf16[128,128]{1,0:T(8,128)(2,1)S(1)}, u32[]{:S(2)}, u32[]{:S(2)}) collective-permute-start(bf16[128,128]{1,0:T(8,128)(2,1)S(1)} %shard_map.113), channel_id=1, source_target_pairs={{256,384},{264,392},{272,400},{280,408},{288,416},{296,424},{304,4... | collective-permute-start | bytes 98312 | tf_op jit(solution)/shard_map/ppermute | solution.py:321
  34.1 10.6 %collective-permute-done.6.third_ref = bf16[128,128]{1,0:T(8,128)(2,1)S(1)} collective-permute-done((bf16[128,128]{1,0:T(8,128)(2,1)S(1)}, bf16[128,128]{1,0:T(8,128)(2,1)S(1)}, u32[]{:S(2)}, u32[]{:S(2)}) %collective-permute-start.6) | collective-permute-done | bytes 32800 | tf_op jit(solution)/shard_map/ppermute | solution.py:321
  44.7 0.0 copy-done.2
  44.7 0.5 shard_map.114
  45.2 8.2 %all_to_all.21.normed_ref = bf16[4,128,128]{2,1,0:T(8,128)(2,1)S(1)} all-to-all(bf16[4,128,128]{2,1,0:T(8,128)(2,1)S(1)} %shard_map.114), channel_id=1, replica_groups={{0,8,16,24},{32,40,48,56},{64,72,80,88},{96,104,112,120},{128,136,144,1..., dimensions={0} | all-to-all | bytes 262144 | tf_op jit(solution)/shard_map/all_to_all | solution.py:284
  53.4 0.0 copy-done
  53.4 0.0 copy-done.1
  53.4 0.5 shard_map.115
  53.9 24.0 %all_to_all.22 = bf16[8,16,2048]{2,1,0:T(8,128)(2,1)S(1)} all-to-all(bf16[8,16,2048]{2,1,0:T(8,128)(2,1)S(1)} %bitcast.4), channel_id=1, replica_groups=mesh['ctx'=64,'head'=8] {'head'}, dimensions={0} | all-to-all | bytes 1048576 | tf_op jit(solution)/shard_map/all_to_all | solution.py:333
  77.9 0.7 reduce_sum.12
Async XLA Ops:
  0.0 53.4 %copy-start = (bf16[512,2048]{1,0:T(8,128)(2,1)S(1)}, bf16[512,2048]{1,0:T(8,128)(2,1)}, u32[]{:S(2)}) copy-start(bf16[512,2048]{1,0:T(8,128)(2,1)} %weight_ref) | copy-start | bytes 6291460
  0.0 53.4 %copy-start.1 = (bf16[128,512]{1,0:T(8,128)(2,1)S(1)}, bf16[128,512]{1,0:T(8,128)(2,1)}, u32[]{:S(2)}) copy-start(bf16[128,512]{1,0:T(8,128)(2,1)} %gate_ref) | copy-start | bytes 393220
  0.0 44.7 %copy-start.2 = (f32[128]{0:T(128)S(1)}, f32[128]{0:T(128)}, u32[]{:S(2)}) copy-start(f32[128]{0:T(128)} %param.20) | copy-start | bytes 1540
  2.7 11.1 %all-to-all-start = ((bf16[4,400,128]{2,1,0:T(8,128)(2,1)}), bf16[4,400,128]{2,1,0:T(8,128)(2,1)S(1)}, u32[]{:S(2)}, u32[]{:S(2)}) async-start(bf16[4,400,128]{2,1,0:T(8,128)(2,1)} %get-tuple-element.20), calls=%async_computation | async-start | bytes 819200 | tf_op jit(solution)/shard_map/all_to_all | solution.py:284
  6.2 7.6 %collective-permute-start = (bf16[16,384]{1,0:T(8,128)(2,1)S(1)}, bf16[16,384]{1,0:T(8,128)(2,1)S(1)}, u32[]{:S(2)}, u32[]{:S(2)}) collective-permute-start(bf16[16,384]{1,0:T(8,128)(2,1)S(1)} %get-tuple-element.23), channel_id=1, source_target_pairs={{24,32},{56,64},{88,96},{120,128},{152,160},{184,192},{216,224},{2... | collective-permute-start | bytes 36872 | tf_op jit(solution)/shard_map/ppermute | solution.py:298
  7.5 6.3 %collective-permute-start.1 = (bf16[16,384]{1,0:T(8,128)(2,1)S(1)}, bf16[16,384]{1,0:T(8,128)(2,1)S(1)}, u32[]{:S(2)}, u32[]{:S(2)}) collective-permute-start(bf16[16,384]{1,0:T(8,128)(2,1)S(1)} %get-tuple-element.24), channel_id=1, source_target_pairs={{24,40},{56,72},{88,104},{120,136},{152,168},{184,200},{216,232},{... | collective-permute-start | bytes 36872 | tf_op jit(solution)/shard_map/ppermute | solution.py:298
  8.1 5.6 %collective-permute-start.2 = (bf16[16,384]{1,0:T(8,128)(2,1)S(1)}, bf16[16,384]{1,0:T(8,128)(2,1)S(1)}, u32[]{:S(2)}, u32[]{:S(2)}) collective-permute-start(bf16[16,384]{1,0:T(8,128)(2,1)S(1)} %get-tuple-element.25), channel_id=1, source_target_pairs={{24,48},{56,80},{88,112},{120,144},{152,176},{184,208},{216,240},{... | collective-permute-start | bytes 36872 | tf_op jit(solution)/shard_map/ppermute | solution.py:298
  8.8 5.0 %collective-permute-start.3 = (bf16[16,384]{1,0:T(8,128)(2,1)S(1)}, bf16[16,384]{1,0:T(8,128)(2,1)S(1)}, u32[]{:S(2)}, u32[]{:S(2)}) collective-permute-start(bf16[16,384]{1,0:T(8,128)(2,1)S(1)} %get-tuple-element.26), channel_id=1, source_target_pairs={{24,56},{56,88},{88,120},{120,152},{152,184},{184,216},{216,248},{... | collective-permute-start | bytes 36872 | tf_op jit(solution)/shard_map/ppermute | solution.py:298
  31.2 0.7 collective-permute-start.4
  32.0 0.7 collective-permute-start.5
  32.8 11.9 %collective-permute-start.6 = (bf16[128,128]{1,0:T(8,128)(2,1)S(1)}, bf16[128,128]{1,0:T(8,128)(2,1)S(1)}, u32[]{:S(2)}, u32[]{:S(2)}) collective-permute-start(bf16[128,128]{1,0:T(8,128)(2,1)S(1)} %shard_map.113), channel_id=1, source_target_pairs={{256,384},{264,392},{272,400},{280,408},{288,416},{296,424},{304,4... | collective-permute-start | bytes 98312 | tf_op jit(solution)/shard_map/ppermute | solution.py:321

commit v6 on v4

--- a/solution.py
+++ b/solution.py
@@ -239,6 +239,13 @@
     ).astype(BF16)
 
 
+def sum_kernel(parts_ref, out_ref):
+    total = parts_ref[0].astype(F32)
+    for i in range(1, parts_ref.shape[0]):
+        total = total + parts_ref[i].astype(F32)
+    out_ref[...] = total.astype(BF16)
+
+
 def call(body, outs, *args, **more):
     return pl.pallas_call(
         body,
@@ -330,7 +337,7 @@
     normed = trade(normed, near)
     partial = call(project_kernel, shape((length, width), BF16), normed, output_gate, out_weight)
     partial = lax.all_to_all(partial.reshape(heads, length // heads, width), "head", 0, 0)
-    return jnp.sum(partial.astype(F32), axis=0).astype(BF16)
+    return call(sum_kernel, shape(partial.shape[1:], BF16), partial)
 
 
 def solution(mesh):

time: 79 us -> 79 us (level)
    pallas_call x7 -> x8, Pallas kernels: 9.09 us -> 9.79 us  [call(): pl.pallas_call(body, out_shape=outs, compiler_params=pltpu.CompilerParams...]
where the time goes in v6:
time: 79 us; the launch traced here: 78.6 us
  blocking collectives  44.5 us (56%)
  waiting for transfers between devices  14.9 us (19%)
  Pallas kernels  9.79 us (12%)
  starting transfers between devices  9.36 us (12%)
    all_to_all x1, blocking collectives, local(): lax.all_to_all(partial.reshape(heads, length // heads, width), 'head', 0, 0)  24 us
    all_to_all x2, blocking collectives, trade(): return lax.all_to_all(a, 'ctx', 0, 0, axis_index_groups=groups)  20.4 us
    ppermute x3, waiting for transfers between devices, local(): states.append(lax.ppermute(leaving, 'ctx', pairs))  10.6 us
    pallas_call x8, Pallas kernels, call(): pl.pallas_call(body, out_shape=outs, compiler_params=pltpu.CompilerParams...  9.79 us
    all_to_all x1, waiting for transfers between devices, trade(): return lax.all_to_all(a, 'ctx', 0, 0, axis_index_groups=groups)  4.27 us
    all_to_all x1, starting transfers between devices, trade(): return lax.all_to_all(a, 'ctx', 0, 0, axis_index_groups=groups)  3.47 us
    ppermute x4, starting transfers between devices, local(): lax.ppermute(rim, 'ctx', [(i, i + 1 + h) for i in range(GROUP - 1, device...  3.28 us
    ppermute x3, starting transfers between devices, local(): states.append(lax.ppermute(leaving, 'ctx', pairs))  2.61 us
  transfers between devices with their start and end apart: 8, of which 2 were waited for; matrix products, arithmetic and copies ran while one was open for 0% of the time, Pallas kernels for 0%

profile of v6, /device:TPU:384, one launch (start us, length us, event | category | flops | bytes accessed | tf_op | source)
XLA Modules:
  0.0 78.6 jit_solution(6884778562099813499)
XLA Ops:
  0.0 0.0 copy-start
  0.0 0.0 copy-start.1
  0.0 0.0 copy-start.2
  0.0 2.7 %shard_map.109 = (bf16[4,400,128]{2,1,0:T(8,128)(2,1)}, f32[16,128]{1,0:T(8,128)S(1)}, bf16[16,384]{1,0:T(8,128)(2,1)S(1)}, bf16[16,384]{1,0:T(8,128)(2,1)S(1)},...) custom-call(bf16[128,256]{1,0:T(8,128)(2,1)} %q_hbm.1, bf16[128,256]{1,0:T(8,128)(2,1)} %k_hbm.1, ...), custom_call_target="tpu_custom_call" | custom-call | tf_op jit(solution)/shard_map/pallas_call | solution.py:250
  2.7 3.5 %all-to-all-start = ((bf16[4,400,128]{2,1,0:T(8,128)(2,1)}), bf16[4,400,128]{2,1,0:T(8,128)(2,1)S(1)}, u32[]{:S(2)}, u32[]{:S(2)}) async-start(bf16[4,400,128]{2,1,0:T(8,128)(2,1)} %get-tuple-element.20), calls=%async_computation | async-start | bytes 819200 | tf_op jit(solution)/shard_map/all_to_all | solution.py:290
  6.2 1.3 %collective-permute-start = (bf16[16,384]{1,0:T(8,128)(2,1)S(1)}, bf16[16,384]{1,0:T(8,128)(2,1)S(1)}, u32[]{:S(2)}, u32[]{:S(2)}) collective-permute-start(bf16[16,384]{1,0:T(8,128)(2,1)S(1)} %get-tuple-element.23), channel_id=1, source_target_pairs={{24,32},{56,64},{88,96},{120,128},{152,160},{184,192},{216,224},{2... | collective-permute-start | bytes 36872 | tf_op jit(solution)/shard_map/ppermute | solution.py:304
  7.5 0.7 collective-permute-start.1
  8.1 0.7 collective-permute-start.2
  8.8 0.7 collective-permute-start.3
  9.5 4.3 %all-to-all-done.msg_ref = bf16[4,400,128]{2,1,0:T(8,128)(2,1)S(1)} async-done(((bf16[4,400,128]{2,1,0:T(8,128)(2,1)}), bf16[4,400,128]{2,1,0:T(8,128)(2,1)S(1)}, u32[]{:S(2)}, u32[]{:S(2)}) %all-to-all-start) | async-done | bytes 409632 | tf_op jit(solution)/shard_map/all_to_all | solution.py:290
  13.8 0.0 collective-permute-done.rim0
  13.8 0.0 collective-permute-done.1.rim1
  13.8 0.0 collective-permute-done.2.rim2
  13.8 0.0 collective-permute-done.3.rim3
  13.8 4.6 %shard_map.110 = (bf16[4,256,128]{2,1,0:T(8,128)(2,1)S(1)}, f32[512,128]{1,0:T(8,128)S(1)}, bf16[512,128]{1,0:T(8,128)(2,1)S(1)}) custom-call(bf16[4,400,128]{2,1,0:T(8,128)(2,1)S(1)} %all-to-all-done.msg_ref, f32[16,128]{1,0:T(8,128)S(1)} %get-tuple-element.22.taps_ref, bf16[16,384]{1,0:T(8,128)(2,1)S(1)} %collective-permute-done.rim0, ...), custom_call_target="tpu_custom_call" | custom-call | tf_op jit(solution)/shard_map/pallas_call | solution.py:250
  18.4 12.2 %all_to_all.20.maps_ref = bf16[4,256,128]{2,1,0:T(8,128)(2,1)S(1)} all-to-all(bf16[4,256,128]{2,1,0:T(8,128)(2,1)S(1)} %get-tuple-element.27), channel_id=1, replica_groups={{0,32,64,96},{8,40,72,104},{16,48,80,112},{24,56,88,120},{128,160,192,2..., dimensions={0} | all-to-all | bytes 524288 | tf_op jit(solution)/shard_map/all_to_all | solution.py:290
  30.6 0.5 shard_map.111
  31.2 0.7 collective-permute-start.4
  31.9 0.0 collective-permute-done.4.refs_0_.first_ref
  31.9 0.1 shard_map.112
  32.0 0.7 collective-permute-start.5
  32.7 0.0 collective-permute-done.5.refs_1_.second_ref
  32.7 0.1 shard_map.113
  32.8 1.3 %collective-permute-start.6 = (bf16[128,128]{1,0:T(8,128)(2,1)S(1)}, bf16[128,128]{1,0:T(8,128)(2,1)S(1)}, u32[]{:S(2)}, u32[]{:S(2)}) collective-permute-start(bf16[128,128]{1,0:T(8,128)(2,1)S(1)} %shard_map.113), channel_id=1, source_target_pairs={{256,384},{264,392},{272,400},{280,408},{288,416},{296,424},{304,4... | collective-permute-start | bytes 98312 | tf_op jit(solution)/shard_map/ppermute | solution.py:327
  34.1 10.6 %collective-permute-done.6.third_ref = bf16[128,128]{1,0:T(8,128)(2,1)S(1)} collective-permute-done((bf16[128,128]{1,0:T(8,128)(2,1)S(1)}, bf16[128,128]{1,0:T(8,128)(2,1)S(1)}, u32[]{:S(2)}, u32[]{:S(2)}) %collective-permute-start.6) | collective-permute-done | bytes 32800 | tf_op jit(solution)/shard_map/ppermute | solution.py:327
  44.7 0.0 copy-done.2
  44.7 0.5 shard_map.114
  45.2 8.2 %all_to_all.21.normed_ref = bf16[4,128,128]{2,1,0:T(8,128)(2,1)S(1)} all-to-all(bf16[4,128,128]{2,1,0:T(8,128)(2,1)S(1)} %shard_map.114), channel_id=1, replica_groups={{0,8,16,24},{32,40,48,56},{64,72,80,88},{96,104,112,120},{128,136,144,1..., dimensions={0} | all-to-all | bytes 262144 | tf_op jit(solution)/shard_map/all_to_all | solution.py:290
  53.4 0.0 copy-done
  53.4 0.0 copy-done.1
  53.4 0.5 shard_map.115
  53.9 24.0 %all_to_all.22.parts_ref = bf16[8,16,2048]{2,1,0:T(8,128)(2,1)S(1)} all-to-all(bf16[8,16,2048]{2,1,0:T(8,128)(2,1)S(1)} %bitcast.4), channel_id=1, replica_groups=mesh['ctx'=64,'head'=8] {'head'}, dimensions={0} | all-to-all | bytes 1048576 | tf_op jit(solution)/shard_map/all_to_all | solution.py:339
  77.9 0.7 shard_map.116
Async XLA Ops:
  0.0 53.4 %copy-start = (bf16[512,2048]{1,0:T(8,128)(2,1)S(1)}, bf16[512,2048]{1,0:T(8,128)(2,1)}, u32[]{:S(2)}) copy-start(bf16[512,2048]{1,0:T(8,128)(2,1)} %weight_ref) | copy-start | bytes 6291460
  0.0 53.4 %copy-start.1 = (bf16[128,512]{1,0:T(8,128)(2,1)S(1)}, bf16[128,512]{1,0:T(8,128)(2,1)}, u32[]{:S(2)}) copy-start(bf16[128,512]{1,0:T(8,128)(2,1)} %gate_ref) | copy-start | bytes 393220
  0.0 44.7 %copy-start.2 = (f32[128]{0:T(128)S(1)}, f32[128]{0:T(128)}, u32[]{:S(2)}) copy-start(f32[128]{0:T(128)} %param.20) | copy-start | bytes 1540
  2.7 11.1 %all-to-all-start = ((bf16[4,400,128]{2,1,0:T(8,128)(2,1)}), bf16[4,400,128]{2,1,0:T(8,128)(2,1)S(1)}, u32[]{:S(2)}, u32[]{:S(2)}) async-start(bf16[4,400,128]{2,1,0:T(8,128)(2,1)} %get-tuple-element.20), calls=%async_computation | async-start | bytes 819200 | tf_op jit(solution)/shard_map/all_to_all | solution.py:290
  6.2 7.6 %collective-permute-start = (bf16[16,384]{1,0:T(8,128)(2,1)S(1)}, bf16[16,384]{1,0:T(8,128)(2,1)S(1)}, u32[]{:S(2)}, u32[]{:S(2)}) collective-permute-start(bf16[16,384]{1,0:T(8,128)(2,1)S(1)} %get-tuple-element.23), channel_id=1, source_target_pairs={{24,32},{56,64},{88,96},{120,128},{152,160},{184,192},{216,224},{2... | collective-permute-start | bytes 36872 | tf_op jit(solution)/shard_map/ppermute | solution.py:304
  7.5 6.3 %collective-permute-start.1 = (bf16[16,384]{1,0:T(8,128)(2,1)S(1)}, bf16[16,384]{1,0:T(8,128)(2,1)S(1)}, u32[]{:S(2)}, u32[]{:S(2)}) collective-permute-start(bf16[16,384]{1,0:T(8,128)(2,1)S(1)} %get-tuple-element.24), channel_id=1, source_target_pairs={{24,40},{56,72},{88,104},{120,136},{152,168},{184,200},{216,232},{... | collective-permute-start | bytes 36872 | tf_op jit(solution)/shard_map/ppermute | solution.py:304
  8.1 5.6 %collective-permute-start.2 = (bf16[16,384]{1,0:T(8,128)(2,1)S(1)}, bf16[16,384]{1,0:T(8,128)(2,1)S(1)}, u32[]{:S(2)}, u32[]{:S(2)}) collective-permute-start(bf16[16,384]{1,0:T(8,128)(2,1)S(1)} %get-tuple-element.25), channel_id=1, source_target_pairs={{24,48},{56,80},{88,112},{120,144},{152,176},{184,208},{216,240},{... | collective-permute-start | bytes 36872 | tf_op jit(solution)/shard_map/ppermute | solution.py:304
  8.8 5.0 %collective-permute-start.3 = (bf16[16,384]{1,0:T(8,128)(2,1)S(1)}, bf16[16,384]{1,0:T(8,128)(2,1)S(1)}, u32[]{:S(2)}, u32[]{:S(2)}) collective-permute-start(bf16[16,384]{1,0:T(8,128)(2,1)S(1)} %get-tuple-element.26), channel_id=1, source_target_pairs={{24,56},{56,88},{88,120},{120,152},{152,184},{184,216},{216,248},{... | collective-permute-start | bytes 36872 | tf_op jit(solution)/shard_map/ppermute | solution.py:304
  31.2 0.7 collective-permute-start.4
  32.0 0.7 collective-permute-start.5
  32.8 11.9 %collective-permute-start.6 = (bf16[128,128]{1,0:T(8,128)(2,1)S(1)}, bf16[128,128]{1,0:T(8,128)(2,1)S(1)}, u32[]{:S(2)}, u32[]{:S(2)}) collective-permute-start(bf16[128,128]{1,0:T(8,128)(2,1)S(1)} %shard_map.113), channel_id=1, source_target_pairs={{256,384},{264,392},{272,400},{280,408},{288,416},{296,424},{304,4... | collective-permute-start | bytes 98312 | tf_op jit(solution)/shard_map/ppermute | solution.py:327
